TPU v7x, 32 devices: a whole 2x2x4 slice. The times are simulated.
32 devices in a mesh: section: 2 (over y), dp: 16 (over z, x, core).
Axes of the slice: x: 2, y: 2, z: 4, core: 2. Of those that a mesh axis runs over, the one named last changes fastest.
Arguments:
- token_ids: int32 [32, 128], P('dp'), may hold values from 0 to 4095
- target_ids: int32 [32, 128], P('dp'), may hold values from 0 to 4095
- segment_ids: int32 [32, 128], P('dp'), may hold values from 0 to 3, never falling along the last dimension, each value on 1 to 64 neighbouring positions
- token_embed: bfloat16 [4096, 768], P('dp'), may hold values from -0.41992188 to 0.41992188
- pos_embed: bfloat16 [1024, 768], replicated, may hold values from -0.59765625 to 0.59765625
- final_gain: bfloat16 [768], replicated, may hold values from 0.5 to 1.5
- final_bias: bfloat16 [768], replicated, may hold values from -1 to 1
- ln1_gain: bfloat16 [2, 768], P('section'), may hold values from 0.5 to 1.5
- ln1_bias: bfloat16 [2, 768], P('section'), may hold values from -1 to 1
- qkv_weight: bfloat16 [2, 768, 2304], P('section'), may hold values from -0.21875 to 0.21875
- qv_bias: bfloat16 [2, 1536], P('section'), may hold values from -1 to 1
- out_weight: bfloat16 [2, 768, 768], P('section'), may hold values from -0.625 to 0.625
- out_bias: bfloat16 [2, 768], P('section'), may hold values from -1 to 1
- ln2_gain: bfloat16 [2, 768], P('section'), may hold values from 0.5 to 1.5
- ln2_bias: bfloat16 [2, 768], P('section'), may hold values from -1 to 1
- fc_weight: bfloat16 [2, 768, 3072], P('section'), may hold values from -0.21875 to 0.21875
- fc_bias: bfloat16 [2, 3072], P('section'), may hold values from -1 to 1
- proj_weight: bfloat16 [2, 3072, 768], P('section'), may hold values from -0.109375 to 0.109375
- proj_bias: bfloat16 [2, 768], P('section'), may hold values from -1 to 1
Outputs:
- loss: float32 [], replicated
- grad_token_embed: float32 [4096, 768], P('dp')
- grad_pos_embed: float32 [1024, 768], P('dp')
- grad_final_gain: float32 [768], P('dp')
- grad_final_bias: float32 [768], P('dp')
- grad_ln1_gain: float32 [2, 768], P('section', 'dp')
- grad_ln1_bias: float32 [2, 768], P('section', 'dp')
- grad_qkv_weight: float32 [2, 768, 2304], P('section', 'dp')
- grad_qv_bias: float32 [2, 1536], P('section', 'dp')
- grad_out_weight: float32 [2, 768, 768], P('section', 'dp')
- grad_out_bias: float32 [2, 768], P('section', 'dp')
- grad_ln2_gain: float32 [2, 768], P('section', 'dp')
- grad_ln2_bias: float32 [2, 768], P('section', 'dp')
- grad_fc_weight: float32 [2, 768, 3072], P('section', 'dp')
- grad_fc_bias: float32 [2, 3072], P('section', 'dp')
- grad_proj_weight: float32 [2, 3072, 768], P('section', 'dp')
- grad_proj_bias: float32 [2, 768], P('section', 'dp')
Inputs may be any that keep to these rules, and one draw needn't show every extreme that they name: `segment_ids`: segment numbers never fall along a row; each segment holds 1 to 64 positions.
All inputs are finite; a program needn't handle non-finite values.
Results may differ from a plain program's by a relative error of at most 0.0035.
Values may be sent and summed in bfloat16 or wider, within the bound.
No kernel may reach another device: no remote copies, remote signals or barrier semaphores. Data moves between devices by JAX's collectives and lax.ppermute only.
A program may use at most 512 MiB of HBM per device.

v0:
```python
import math

import jax
import jax.numpy as jnp
from jax import lax
from jax.experimental import pallas as pl
from jax.experimental.pallas import tpu as pltpu
from jax.sharding import PartitionSpec as P


HEADS = 12
HD = 64
BF = jnp.bfloat16
F32 = jnp.float32
META = 128
VMEM_LIMIT = 60 * 1024 * 1024


def nn(left, right):
    return lax.dot_general(left, right, (((1,), (0,)), ((), ())), preferred_element_type=F32)


def nt(left, right):
    return lax.dot_general(left, right, (((1,), (1,)), ((), ())), preferred_element_type=F32)


def tn(left, right):
    return lax.dot_general(left, right, (((0,), (0,)), ((), ())), preferred_element_type=F32)


def normalised(values):
    centre = jnp.mean(values, axis=-1, keepdims=True)
    shifted = values - centre
    spread = jnp.mean(shifted * shifted, axis=-1, keepdims=True)
    scale = lax.rsqrt(spread + 1e-05)
    return shifted * scale, scale


def norm_back(grad, gain, hat, scale):
    ghat = grad * gain
    first = jnp.mean(ghat, axis=-1, keepdims=True)
    second = jnp.mean(ghat * hat, axis=-1, keepdims=True)
    return scale * (ghat - first - hat * second)


def rowsum(values):
    return jnp.sum(values, axis=0, keepdims=True)


TANH_SCALE = math.sqrt(2.0 / math.pi)


def gelu_parts(inner):
    square = inner * inner
    bend = jnp.tanh(TANH_SCALE * (inner + 0.044715 * (square * inner)))
    return 0.5 * (1.0 + bend), bend, square


def pair_masks(length):
    lane = lax.broadcasted_iota(jnp.int32, (length, 2 * HD), 1)
    return lane < HD


def stacked(values, even):
    zero = jnp.zeros_like(values)
    return jnp.concatenate(
        [jnp.where(even, values, zero), jnp.where(even, zero, values)], axis=0
    )


def pair_probs(queries, key_stack, allowed, length):
    scores = nt(queries, key_stack) * HD ** (-0.5)
    probs = []
    for part in range(2):
        own = jnp.where(allowed, scores[:, part * length : (part + 1) * length], -1e30)
        peak = jnp.max(own, axis=-1, keepdims=True)
        raised = jnp.exp(own - peak)
        probs.append(raised * (1.0 / jnp.sum(raised, axis=-1, keepdims=True)))
    return probs


def allowed_of(segc_ref, segr_ref, seq, length):
    rows = lax.broadcasted_iota(jnp.int32, (length, length), 0)
    cols = lax.broadcasted_iota(jnp.int32, (length, length), 1)
    same = segc_ref[pl.ds(seq * length, length), :] == segr_ref[pl.ds(seq, 1), :]
    return (rows >= cols) & same


def start_copies(pairs, sems):
    copies = [pltpu.make_async_copy(src, dst, sems.at[i]) for i, (src, dst) in enumerate(pairs)]
    for copy in copies:
        copy.start()
    return copies


def forward_kernel(
    x_ref, segc_ref, segr_ref, g1, b1, bqkv, bo, g2, b2, bfc, bproj,
    wqkv_h, wo_h, wfc_h, wproj_h, *rest, save,
):
    width = x_ref.shape[1]
    if save:
        come_ref, first, y_ref, hid_ref, acts_ref, qkv_ref, x1_ref, inner_ref, act_ref = rest[:9]
        att_at = width
        wqkv, wo, wfc, wproj, sems = rest[9:]
    else:
        y_ref, qkv_ref, acts_ref, wqkv, wo, wfc, wproj, sems = rest
        att_at = 0
    copies = start_copies(
        ((wqkv_h.at[0], wqkv), (wo_h.at[0], wo), (wfc_h.at[0], wfc), (wproj_h.at[0], wproj)), sems
    )
    micro, length = segr_ref.shape
    hidden = x_ref[...]
    if save:
        hidden = jnp.where(first[0] == 1, hidden, come_ref[...].astype(F32))
        hid_ref[...] = hidden
    hat, _ = normalised(hidden)
    a1 = (hat * wide(g1) + wide(b1)).astype(BF)
    if save:
        acts_ref[:, :width] = a1
    copies[0].wait()
    for part in range(3):
        cols = slice(part * width, (part + 1) * width)
        qkv_ref[:, cols] = (nn(a1, wqkv[:, cols]) + bqkv[:, cols].astype(F32)).astype(BF)
    even = pair_masks(length)
    for seq in range(micro):
        allowed = allowed_of(segc_ref, segr_ref, seq, length)
        rows = slice(seq * length, (seq + 1) * length)
        for pair in range(HEADS // 2):
            lo = pair * 2 * HD
            queries = qkv_ref[rows, lo : lo + 2 * HD]
            key_stack = stacked(qkv_ref[rows, width + lo : width + lo + 2 * HD], even)
            value_stack = stacked(qkv_ref[rows, 2 * width + lo : 2 * width + lo + 2 * HD], even)
            probs = pair_probs(queries, key_stack, allowed, length)
            joined = jnp.concatenate([part.astype(BF) for part in probs], axis=1)
            acts_ref[rows, att_at + lo : att_at + lo + 2 * HD] = nn(joined, value_stack).astype(BF)
    copies[1].wait()
    x1 = hidden + nn(acts_ref[:, att_at : att_at + width], wo[...]) + wide(bo)
    hat2, _ = normalised(x1)
    a2 = (hat2 * wide(g2) + wide(b2)).astype(BF)
    if save:
        x1_ref[...] = x1
        acts_ref[:, 2 * width :] = a2
    copies[2].wait()
    copies[3].wait()
    total = x1 + wide(bproj)
    hidden_units = wfc.shape[1]
    for part in range(hidden_units // width):
        cols = slice(part * width, (part + 1) * width)
        inner = nn(a2, wfc[:, cols]) + bfc[:, cols].astype(F32)
        half, _, _ = gelu_parts(inner)
        act = (inner * half).astype(BF)
        if save:
            inner_ref[:, cols] = inner
            act_ref[:, cols] = act
        total = total + nn(act, wproj[cols, :])
    y_ref[...] = total.astype(y_ref.dtype)


def wide(ref):
    return ref[...].astype(F32)


def any_spec():
    return pl.BlockSpec(memory_space=pl.ANY)


def vmem_spec():
    return pl.BlockSpec(memory_space=pltpu.VMEM)


def smem_spec():
    return pl.BlockSpec(memory_space=pltpu.SMEM)


def params():
    return pltpu.CompilerParams(vmem_limit_bytes=VMEM_LIMIT)


def forward_layer(hidden, seg_col, seg_row, vectors, weights, incoming=None, first=None):
    save = incoming is not None
    rows, width = hidden.shape
    units = weights[2].shape[2]
    span = weights[0].shape[2]
    sds = jax.ShapeDtypeStruct
    if save:
        outs = [
            sds((rows, width), F32), sds((rows, width), F32), sds((rows, 3 * width), BF),
            sds((rows, span), BF), sds((rows, width), F32), sds((rows, units), F32),
            sds((rows, units), BF),
        ]
        scratch = []
        extra, extra_specs = (incoming, first), [vmem_spec(), smem_spec()]
    else:
        outs = [sds((rows, width), BF)]
        scratch = [pltpu.VMEM((rows, span), BF), pltpu.VMEM((rows, width), BF)]
        extra, extra_specs = (), []
    scratch = scratch + [pltpu.VMEM(w.shape[1:], BF) for w in weights]
    scratch.append(pltpu.SemaphoreType.DMA((4,)))

    def kernel(*refs):
        forward_kernel(*refs, save=save)

    return pl.pallas_call(
        kernel,
        out_shape=outs,
        in_specs=[vmem_spec()] * 11 + [any_spec()] * 4 + extra_specs,
        out_specs=[vmem_spec()] * len(outs),
        scratch_shapes=scratch,
        compiler_params=params(),
        name="layer_forward_save" if save else "layer_forward",
    )(hidden, seg_col, seg_row, *vectors, *weights, *extra)


def mlp_back_kernel(dy_ref, x1_ref, inner_ref, g2, wfc_h, wproj_h, *rest, save):
    if save:
        gy_ref, first, dx1_ref, gin_ref, dg2, db2, dfc, dproj, wfc, wproj, sems = rest
    else:
        dx1_ref, wfc, wproj, sems = rest
    copies = start_copies(((wproj_h.at[0], wproj), (wfc_h.at[0], wfc)), sems)
    width = dy_ref.shape[1]
    units = inner_ref.shape[1]
    dy = dy_ref[...]
    if save:
        gy = gy_ref[...]
        dy = jnp.where(first[0] == 1, gy.astype(F32), dy)
        dproj[...] = rowsum(dy)
    else:
        gy = dy.astype(BF)
    hat, scale = normalised(x1_ref[...])
    copies[0].wait()
    copies[1].wait()
    da2 = jnp.zeros(dy.shape, F32)
    for part in range(units // width):
        cols = slice(part * width, (part + 1) * width)
        dact = nt(gy, wproj[cols, :])
        inner = inner_ref[:, cols]
        half, bend, square = gelu_parts(inner)
        slope = half + (0.5 * TANH_SCALE) * inner * (1.0 - bend * bend) * (
            1.0 + (3 * 0.044715) * square
        )
        gin = (dact * slope).astype(BF)
        if save:
            gin_ref[:, cols] = gin
            dfc[:, cols] = rowsum(gin.astype(F32))
        da2 = da2 + nt(gin, wfc[:, cols])
    if save:
        dg2[...] = rowsum(da2 * hat)
        db2[...] = rowsum(da2)
    dx1_ref[...] = dy + norm_back(da2, wide(g2), hat, scale)


def mlp_back(dy, x1, inner, gain, wfc, wproj, gy=None, first=None):
    save = gy is not None
    rows, width = dy.shape
    units = inner.shape[1]
    sds = jax.ShapeDtypeStruct
    outs = [sds((rows, width), F32)]
    extra, extra_specs = (), []
    if save:
        outs += [
            sds((rows, units), BF), sds((1, width), F32), sds((1, width), F32),
            sds((1, units), F32), sds((1, width), F32),
        ]
        extra, extra_specs = (gy, first), [vmem_spec(), smem_spec()]

    def kernel(*refs):
        mlp_back_kernel(*refs, save=save)

    return pl.pallas_call(
        kernel,
        out_shape=outs,
        in_specs=[vmem_spec()] * 4 + [any_spec()] * 2 + extra_specs,
        out_specs=[vmem_spec()] * len(outs),
        scratch_shapes=[
            pltpu.VMEM(wfc.shape[1:], BF), pltpu.VMEM(wproj.shape[1:], BF),
            pltpu.SemaphoreType.DMA((2,)),
        ],
        compiler_params=params(),
        name="mlp_back_save" if save else "mlp_back",
    )(dy, x1, inner, gain, wfc, wproj, *extra)


def att_back_kernel(dx1_ref, x_ref, qkv_ref, segc_ref, segr_ref, g1, wqkv_h, wo_h, *rest, save):
    if save:
        meta_ref, dx_ref, grads_ref, dg1, db1, dbqkv, dbo, datt_ref, wqkv, wo, sems = rest
    else:
        dx_ref, grads_ref, datt_ref, wqkv, wo, sems = rest
    copies = start_copies(((wo_h.at[0], wo), (wqkv_h.at[0], wqkv)), sems)
    micro, length = segr_ref.shape
    width = x_ref.shape[1]
    dx1 = dx1_ref[...]
    gx1 = dx1.astype(BF)
    if save:
        grads_ref[:, 3 * width :] = gx1
        dbo[...] = rowsum(dx1)
    copies[0].wait()
    datt_ref[...] = nt(gx1, wo[...]).astype(BF)
    even = pair_masks(length)
    for seq in range(micro):
        allowed = allowed_of(segc_ref, segr_ref, seq, length)
        rows = slice(seq * length, (seq + 1) * length)
        for pair in range(HEADS // 2):
            lo = pair * 2 * HD
            queries = qkv_ref[rows, lo : lo + 2 * HD]
            key_stack = stacked(qkv_ref[rows, width + lo : width + lo + 2 * HD], even)
            value_stack = stacked(qkv_ref[rows, 2 * width + lo : 2 * width + lo + 2 * HD], even)
            probs = pair_probs(queries, key_stack, allowed, length)
            dmix = datt_ref[rows, lo : lo + 2 * HD]
            dprobs = nt(dmix, value_stack)
            low = []
            dscores = []
            for part in range(2):
                dp = dprobs[:, part * length : (part + 1) * length]
                inside = jnp.sum(probs[part] * dp, axis=-1, keepdims=True)
                ds = probs[part] * (dp - inside)
                dscores.append((ds * HD ** (-0.5)).astype(BF))
                low.append(probs[part].astype(BF))
            dq = nn(jnp.concatenate(dscores, axis=1), key_stack)
            dk = tn(jnp.concatenate(dscores, axis=0), stacked(queries, even))
            dv = tn(jnp.concatenate(low, axis=0), stacked(dmix, even))
            grads_ref[rows, lo : lo + 2 * HD] = dq.astype(BF)
            grads_ref[rows, width + lo : width + lo + 2 * HD] = dk.astype(BF)
            grads_ref[rows, 2 * width + lo : 2 * width + lo + 2 * HD] = dv.astype(BF)
    hat, scale = normalised(x_ref[...])
    copies[1].wait()
    da1 = jnp.zeros(dx1.shape, F32)
    for part in range(3):
        cols = slice(part * width, (part + 1) * width)
        piece = grads_ref[:, cols]
        if save:
            dbqkv[:, cols] = rowsum(piece.astype(F32))
        da1 = da1 + nt(piece, wqkv[:, cols])
    if save:
        dg1[...] = rowsum(da1 * hat)
        db1[...] = rowsum(da1)
        dx_ref[:, width:] = meta_ref[...]
    dx_ref[:, :width] = (dx1 + norm_back(da1, wide(g1), hat, scale)).astype(BF)


def att_back(dx1, hidden, qkv, seg_col, seg_row, gain, wqkv, wo, meta=None):
    save = meta is not None
    rows, width = dx1.shape
    span = qkv.shape[1]
    sds = jax.ShapeDtypeStruct
    if save:
        outs = [
            sds((rows, width + META), BF), sds((rows, span + width), BF), sds((1, width), F32),
            sds((1, width), F32), sds((1, span), F32), sds((1, width), F32),
        ]
        scratch = []
        extra, extra_specs = (meta,), [vmem_spec()]
    else:
        outs = [sds((rows, width), BF)]
        scratch = [pltpu.VMEM((rows, span), BF)]
        extra, extra_specs = (), []
    scratch = scratch + [
        pltpu.VMEM((rows, width), BF), pltpu.VMEM(wqkv.shape[1:], BF),
        pltpu.VMEM(wo.shape[1:], BF), pltpu.SemaphoreType.DMA((2,)),
    ]

    def kernel(*refs):
        att_back_kernel(*refs, save=save)

    return pl.pallas_call(
        kernel,
        out_shape=outs,
        in_specs=[vmem_spec()] * 6 + [any_spec()] * 2 + extra_specs,
        out_specs=[vmem_spec()] * len(outs),
        scratch_shapes=scratch,
        compiler_params=params(),
        name="att_back_save" if save else "att_back",
    )(dx1, hidden, qkv, seg_col, seg_row, gain, wqkv, wo, *extra)


def share_kernel(spots, wide_ref, mine_ref, theirs_ref, flat_ref, *, arrays, line):
    _, total = wide_ref.shape
    step = 2 * META
    for at in range(0, total, step):
        flat_ref[at : at + step, :] = wide_ref[:, at : at + step].T
    block = total // arrays // (4 * line)
    for slot in range(2):
        for array in range(arrays):
            for place in range(line):
                start = (array * line + spots[4 + place]) * 4 * block
                goal = ((slot * arrays + array) * line + place) * block
                for which, out in enumerate((mine_ref, theirs_ref)):
                    rows = pl.ds(pl.multiple_of(start + spots[2 * which + slot] * block, 16), block)
                    out[goal : goal + block, :] = flat_ref[rows, :]


def share(spots, saved, arrays, line):
    tokens, total = saved.shape
    block = total // arrays // (4 * line)
    if block % 16:
        flat = saved.T.reshape(arrays, line, 4, block, tokens)
        flat = jnp.take(flat, spots[4:], axis=1)
        picked = [lax.dynamic_index_in_dim(flat, spots[i], 2, keepdims=False) for i in range(4)]
        return (
            jnp.stack(picked[:2]).reshape(total // 2, tokens),
            jnp.stack(picked[2:]).reshape(total // 2, tokens),
        )
    out = jax.ShapeDtypeStruct((total // 2, tokens), BF)

    def kernel(*refs):
        share_kernel(*refs, arrays=arrays, line=line)

    return pl.pallas_call(
        kernel,
        out_shape=[out, out],
        in_specs=[smem_spec(), vmem_spec()],
        out_specs=[vmem_spec()] * 2,
        scratch_shapes=[pltpu.VMEM((total, tokens), BF)],
        compiler_params=params(),
    )(spots, saved)


def product(mine, theirs, grads, other, slot, parts, received=None):
    arrays = parts[0][1]
    rows = mine.shape[0] // (2 * arrays)
    cols = grads.shape[1]
    half = rows // 2

    def kernel(mine_ref, theirs_ref, grads_ref, other_ref, *rest):
        for array, _, at, size in parts:
            start = (slot * arrays + array) * rows
            for low in range(at, at + size, 768):
                these = slice(low, low + 768)
                value = nn(mine_ref[start : start + rows, :], grads_ref[:, these]) + nn(
                    theirs_ref[start : start + rows, :], other_ref[:, these]
                )
                if slot:
                    rest[0][:, these] = value.astype(BF)
                else:
                    value = value + rest[0][:, these].astype(F32)
                    rest[1][:, these] = value[:half]
                    rest[2][:, these] = value[half:].astype(BF)

    extra = () if slot else (received,)
    sds = jax.ShapeDtypeStruct
    outs = [sds((rows, cols), BF)] if slot else [sds((half, cols), F32), sds((half, cols), BF)]
    return pl.pallas_call(
        kernel,
        out_shape=outs,
        in_specs=[vmem_spec()] * (4 + len(extra)),
        out_specs=[vmem_spec()] * len(outs),
        compiler_params=params(),
    )(mine, theirs, grads, other, *extra)


def head_kernel(
    h_ref, tgt_ref, gain, offset, table_ref,
    dh_ref, ext_ref, dgain, doff, loss_ref,
    logits, top, total, picked, dhn, length,
):
    turn = pl.program_id(0)
    block = pl.program_id(1)
    blocks = pl.num_programs(1)
    rows, width = h_ref.shape
    size = table_ref.shape[0]

    @pl.when((turn == 0) & (block == 0))
    def _():
        hat, _ = normalised(h_ref[...])
        ext_ref[:, :width] = (hat * wide(gain) + wide(offset)).astype(BF)
        top[...] = jnp.full(top.shape, -1e30, F32)
        total[...] = jnp.zeros(total.shape, F32)
        picked[...] = jnp.zeros(picked.shape, F32)
        dhn[...] = jnp.zeros(dhn.shape, F32)

    words = block * size + lax.broadcasted_iota(jnp.int32, (rows, size), 1)
    hits = words == tgt_ref[...]

    @pl.when(turn == 0)
    def _():
        piece = nt(ext_ref[:, :width], table_ref[...])
        logits[block] = piece
        now = jnp.maximum(top[...], jnp.max(piece, axis=1, keepdims=True))
        total[...] = total[...] * jnp.exp(top[...] - now) + jnp.sum(
            jnp.exp(piece - now), axis=1, keepdims=True
        )
        top[...] = now
        picked[...] += jnp.sum(jnp.where(hits, piece, 0.0), axis=1, keepdims=True)

    @pl.when((turn == 1) & (block == 0))
    def _():
        top[...] = top[...] + jnp.log(total[...])
        lse = top[...]
        loss_ref[...] = jnp.sum(lse - picked[...], axis=0, keepdims=True) / length
        high = lse.astype(BF).astype(F32)
        mid = (lse - high).astype(BF).astype(F32)
        low = lse - high - mid
        tgt = tgt_ref[...]
        tgt_high = (tgt >> 8).astype(F32)
        tgt_low = (tgt & 255).astype(F32)
        lane = lax.broadcasted_iota(jnp.int32, (rows, META), 1)
        meta = jnp.zeros((rows, META), F32)
        for index, column in enumerate((high, mid, low, tgt_high, tgt_low)):
            meta = jnp.where(lane == index, column, meta)
        ext_ref[:, width:] = meta.astype(BF)

    @pl.when(turn == 1)
    def _():
        probs = jnp.exp(logits[block] - top[...])
        dlog = ((probs - hits.astype(F32)) / length).astype(BF)
        dhn[...] += nn(dlog, table_ref[...])

    @pl.when((turn == 1) & (block == blocks - 1))
    def _():
        hat, scale = normalised(h_ref[...])
        grad = dhn[...]
        dgain[...] = rowsum(grad * hat)
        doff[...] = rowsum(grad)
        dh_ref[...] = norm_back(grad, wide(gain), hat, scale)


def head(hidden, targets, gain, offset, table, length):
    rows, width = hidden.shape
    vocab = table.shape[0]
    size = math.gcd(vocab, 1024)
    blocks = vocab // size
    sds = jax.ShapeDtypeStruct

    def kernel(*refs):
        head_kernel(*refs, length=length)

    def full(shape):
        return pl.BlockSpec(shape, lambda t, b: (0,) * len(shape))

    outs = [
        sds((rows, width), F32), sds((rows, width + META), BF), sds((1, width), F32),
        sds((1, width), F32), sds((1, 1), F32),
    ]
    return pl.pallas_call(
        kernel,
        grid=(2, blocks),
        out_shape=outs,
        in_specs=[
            full((rows, width)), full((rows, 1)), full((1, width)), full((1, width)),
            pl.BlockSpec((size, width), lambda t, b: (b, 0)),
        ],
        out_specs=[full(out.shape) for out in outs],
        scratch_shapes=[
            pltpu.VMEM((blocks, rows, size), F32), pltpu.VMEM((rows, 1), F32),
            pltpu.VMEM((rows, 1), F32), pltpu.VMEM((rows, 1), F32),
            pltpu.VMEM((rows, width), F32),
        ],
        compiler_params=params(),
        name="head",
    )(hidden, targets, gain, offset, table)


def table_kernel(base_ref, ext_ref, shard_ref, out_ref, *, length):
    width = shard_ref.shape[1]
    size = shard_ref.shape[0]
    rows = ext_ref.shape[0]

    @pl.when(pl.program_id(0) == 0)
    def _():
        out_ref[...] = jnp.zeros(out_ref.shape, F32)

    hn = ext_ref[:, :width]
    meta = ext_ref[:, width:].astype(F32)
    lse = meta[:, 0:1] + meta[:, 1:2] + meta[:, 2:3]
    target = meta[:, 3:4] * 256.0 + meta[:, 4:5]
    words = (base_ref[0] + lax.broadcasted_iota(jnp.int32, (rows, size), 1)).astype(F32)
    probs = jnp.exp(nt(hn, shard_ref[...]) - lse)
    dlog = ((probs - (words == target).astype(F32)) / length).astype(BF)
    out_ref[...] += tn(dlog, hn)


def table_head(base, ext, shard, length):
    rows = ext.shape[0]
    step = math.gcd(rows, 512)
    width = shard.shape[1]

    def kernel(*refs):
        table_kernel(*refs, length=length)

    return pl.pallas_call(
        kernel,
        grid=(rows // step,),
        out_shape=jax.ShapeDtypeStruct(shard.shape, F32),
        in_specs=[
            pl.BlockSpec(memory_space=pltpu.SMEM),
            pl.BlockSpec((step, width + META), lambda r: (r, 0)),
            pl.BlockSpec(shard.shape, lambda r: (0, 0)),
        ],
        out_specs=pl.BlockSpec(shard.shape, lambda r: (0, 0)),
        compiler_params=params(),
        name="table_head",
    )(base, ext, shard)


def lookup_kernel(base_ref, ext_ref, table_out, pos_out):
    width = table_out.shape[1]
    rows = ext_ref.shape[0]

    @pl.when(pl.program_id(0) == 0)
    def _():
        table_out[...] = jnp.zeros(table_out.shape, F32)
        pos_out[...] = jnp.zeros(pos_out.shape, F32)

    dx = ext_ref[:, :width]
    meta = ext_ref[:, width:].astype(F32)
    token = meta[:, 0:1] * 256.0 + meta[:, 1:2]
    place = meta[:, 2:3] * 256.0 + meta[:, 3:4]
    for index, (value, out) in enumerate(((token, table_out), (place, pos_out))):
        size = out.shape[0]
        names = (base_ref[index] + lax.broadcasted_iota(jnp.int32, (rows, size), 1)).astype(F32)
        chosen = (names == value).astype(F32).astype(BF)
        out[...] += tn(chosen, dx)


def lookup_back(bases, ext, table_rows, pos_rows, width):
    rows = ext.shape[0]
    step = math.gcd(rows, 512)
    outs = [
        jax.ShapeDtypeStruct((table_rows, width), F32),
        jax.ShapeDtypeStruct((pos_rows, width), F32),
    ]
    return pl.pallas_call(
        lookup_kernel,
        grid=(rows // step,),
        out_shape=outs,
        in_specs=[
            pl.BlockSpec(memory_space=pltpu.SMEM),
            pl.BlockSpec((step, width + META), lambda r: (r, 0)),
        ],
        out_specs=[pl.BlockSpec(out.shape, lambda r: (0, 0)) for out in outs],
        compiler_params=params(),
        name="lookup_back",
    )(bases, ext)


class Line:
    def __init__(self):
        self.size = lax.axis_size("dp")
        self.line = self.size // 4
        self.index = lax.axis_index("dp")
        self.core = self.index % 2
        self.pair = (self.index // 2) % 2
        self.place = self.index // 4

    def swap(self, array, bit):
        return lax.ppermute(array, "dp", [(i, i ^ bit) for i in range(self.size)])

    def order(self):
        bits = self.line.bit_length() - 1
        turned = [int(format(k, "b").zfill(bits)[::-1], 2) if bits else 0 for k in range(self.line)]
        return [self.place ^ k for k in turned]

    def line_sum(self, kept, sent):
        bit = 1
        while bit < self.line:
            got = self.swap(sent, 4 * bit)
            bit *= 2
            if bit < self.line:
                half = kept.shape[0] // 2
                sent = (kept[half:] + got[half:].astype(F32)).astype(BF)
                kept = kept[:half] + got[:half].astype(F32)
            else:
                kept = kept + got.astype(F32)
        return kept


def body(
    token_ids, target_ids, segment_ids, token_embed, pos_embed, final_gain, final_bias,
    ln1_gain, ln1_bias, qkv_weight, qv_bias, out_weight, out_bias, ln2_gain, ln2_bias,
    fc_weight, fc_bias, proj_weight, proj_bias,
):
    on_first = lax.axis_index("section") == 0
    line = Line()
    micro, length = token_ids.shape
    rows = micro * length
    shard, width = token_embed.shape
    pos_shard = pos_embed.shape[0] // line.size

    full_table = lax.all_gather(token_embed, "dp", axis=0, tiled=True)
    earlier = segment_ids[:, None, :] < segment_ids[:, :, None]
    places = jnp.arange(length, dtype=jnp.int32)[None, :] - jnp.sum(
        earlier.astype(jnp.int32), axis=2
    )
    flat_places = places.reshape(-1)
    flat_ids = token_ids.reshape(-1)
    embedded = jnp.take(full_table, flat_ids, axis=0).astype(F32) + jnp.take(
        pos_embed, flat_places, axis=0
    ).astype(F32)

    seg_col = segment_ids.reshape(rows, 1)
    bqkv = jnp.concatenate(
        [qv_bias[:, :width], jnp.zeros((1, width), qv_bias.dtype), qv_bias[:, width:]], axis=1
    )
    vectors = (ln1_gain, ln1_bias, bqkv, out_bias, ln2_gain, ln2_bias, fc_bias, proj_bias)
    weights = (qkv_weight, out_weight, fc_weight, proj_weight)
    first = on_first.astype(jnp.int32).reshape(1)
    own = line.pair * 2
    other = 2 - own
    spots = jnp.stack(
        [own + line.core, other + line.core, own + 1 - line.core, other + 1 - line.core]
        + line.order()
    ).astype(jnp.int32)
    lane = jnp.arange(META, dtype=jnp.int32)[None, :]
    meta = jnp.zeros((rows, META), F32)
    for index, column in enumerate(
        (flat_ids >> 8, flat_ids & 255, flat_places >> 8, flat_places & 255)
    ):
        meta = jnp.where(lane == index, column.astype(F32)[:, None], meta)
    meta = meta.astype(BF)

    (first_out,) = forward_layer(embedded, seg_col, segment_ids, vectors, weights)
    incoming = lax.ppermute(first_out, "section", [(0, 1)])
    out, hidden, acts, qkv, x1, inner, act = forward_layer(
        embedded, seg_col, segment_ids, vectors, weights, incoming, first
    )
    dh, ext, dgain, doff, loss = head(
        out, target_ids.reshape(rows, 1), final_gain[None], final_bias[None], full_table, length
    )
    half = rows // 2
    ext_moved = lax.ppermute(ext[half:], "section", [(1, 0)])
    ext_own = jnp.where(on_first, ext_moved, ext[:half])
    ext_all = lax.all_gather(ext_own, "dp", axis=0, tiled=True)

    (mid,) = mlp_back(dh, x1, inner, ln2_gain, fc_weight, proj_weight)
    (back,) = att_back(mid, hidden, qkv, seg_col, segment_ids, ln1_gain, qkv_weight, out_weight)
    back_in = lax.ppermute(back, "section", [(1, 0)])

    mine_p, theirs_p = share(spots, act, 1, line.line)
    got_p = line.swap(theirs_p, 1)
    mine_a, theirs_a = share(spots, acts, 3, line.line)
    got_a = line.swap(theirs_a, 1)

    gy = jnp.where(on_first, back_in, dh.astype(BF))
    gy_other = line.swap(gy, 1)
    units = fc_weight.shape[2]
    span = qkv_weight.shape[2]
    proj_parts = ((0, 1, 0, width),)
    fc_parts = ((2, 3, 0, units),)
    att_parts = ((0, 3, 0, span), (1, 3, span, width))
    (proj_sent,) = product(mine_p, got_p, gy, gy_other, 1, proj_parts)
    proj_got = line.swap(proj_sent, 2)
    dx1, gin, dg2, db2, dfc, dproj = mlp_back(
        dh, x1, inner, ln2_gain, fc_weight, proj_weight, gy, first
    )
    gin_other = line.swap(gin, 1)
    (fc_sent,) = product(mine_a, got_a, gin, gin_other, 1, fc_parts)
    fc_got = line.swap(fc_sent, 2)
    dx_ext, grads, dg1, db1, dbqkv, dbo = att_back(
        dx1, hidden, qkv, seg_col, segment_ids, ln1_gain, qkv_weight, out_weight, meta
    )
    grads_other = line.swap(grads, 1)
    (att_sent,) = product(mine_a, got_a, grads, grads_other, 1, att_parts)
    att_got = line.swap(att_sent, 2)
    proj_own = product(mine_p, got_p, gy, gy_other, 0, proj_parts, proj_got)
    proj_share = line.line_sum(*proj_own)
    fc_own = product(mine_a, got_a, gin, gin_other, 0, fc_parts, fc_got)
    fc_share = line.line_sum(*fc_own)
    att_own = product(mine_a, got_a, grads, grads_other, 0, att_parts, att_got)
    att_share = line.line_sum(*att_own)
    qkv_share, out_share = att_share[:, :span], att_share[:, span:]

    base = line.index * shard
    table_part = table_head(base.reshape(1), ext_all, token_embed, length)

    dx_moved = lax.ppermute(dx_ext[half:], "section", [(0, 1)])
    dx_own = jnp.where(on_first, dx_ext[:half], dx_moved)
    dx_all = lax.all_gather(dx_own, "dp", axis=0, tiled=True)
    bases = jnp.stack([base, line.index * pos_shard])
    lookup, pos_part = lookup_back(bases, dx_all, shard, pos_shard, width)

    masked = [jnp.where(on_first, 0.0, v) for v in (dgain, doff)]
    small = [dg1, db1, dbqkv[:, :width], dbqkv[:, 2 * width :], dbo, dg2, db2, dfc, dproj]
    qv = jnp.concatenate(small[2:4], axis=1)
    small = [small[0], small[1], qv] + small[4:] + masked
    widths = [v.shape[1] // line.size for v in small]
    loss_own = jnp.where(on_first, 0.0, loss[0, 0])
    packed = jnp.concatenate(
        [v.reshape(line.size, -1) for v in small] + [jnp.full((line.size, 1), loss_own, F32)],
        axis=1,
    )
    spread = lax.all_to_all(packed, "dp", 0, 0, tiled=True)
    summed = jnp.sum(spread, axis=0)
    pieces = []
    at = 0
    for size in widths:
        pieces.append(summed[at : at + size])
        at += size
    tail = summed[sum(widths[:-2]) :]
    both = [(0, 1), (1, 0)]
    tail = tail + lax.ppermute(tail, "section", both)
    g_fin, b_fin = tail[: widths[-2]], tail[widths[-2] : widths[-2] + widths[-1]]
    loss_value = tail[-1] / (micro * line.size)
    table_sum = table_part + lax.ppermute(table_part, "section", both)
    late = jnp.concatenate([lookup, pos_part], axis=0)
    late = lax.reduce_precision(late, 8, 7)
    late = late + lax.ppermute(late.astype(BF), "section", both).astype(F32)
    table_sum = table_sum + late[:shard]
    pos_sum = late[shard:]
    return (
        loss_value, table_sum, pos_sum, g_fin, b_fin,
        pieces[0][None], pieces[1][None], qkv_share[None], pieces[2][None], out_share[None],
        pieces[3][None], pieces[4][None], pieces[5][None], fc_share[None], pieces[6][None],
        proj_share[None], pieces[7][None],
    )


def solution(mesh):
    in_specs = (
        P("dp", None), P("dp", None), P("dp", None), P("dp", None), P(), P(), P(),
        P("section", None), P("section", None), P("section", None, None), P("section", None),
        P("section", None, None), P("section", None), P("section", None), P("section", None),
        P("section", None, None), P("section", None), P("section", None, None), P("section", None),
    )
    out_specs = (
        P(), P("dp", None), P("dp", None), P("dp"), P("dp"),
        P("section", "dp"), P("section", "dp"), P("section", "dp", None), P("section", "dp"),
        P("section", "dp", None), P("section", "dp"), P("section", "dp"), P("section", "dp"),
        P("section", "dp", None), P("section", "dp"), P("section", "dp", None),
        P("section", "dp"),
    )
    return jax.shard_map(body, mesh=mesh, in_specs=in_specs, out_specs=out_specs, check_vma=False)
```

profile of v0, /device:TPU:0, one launch (start us, length us, event | category | flops | bytes accessed | tf_op | source)
XLA Modules:
  0.0 408.8 jit_solution(17691702098976550436)
XLA Ops:
  8.0 1.5 copy.47.refs_1_.refs_3_
  9.5 0.9 convert_reduce_fusion
  10.5 1.2 gather_fusion.1
  12.4 62.1 %all-gather.4.cloned.1.call-done.refs_4_ = bf16[4096,768]{1,0:T(8,128)(2,1)} async-done(((bf16[256,768]{1,0:T(8,128)(2,1)}), bf16[4096,768]{1,0:T(8,128)(2,1)}) %all-gather.4.cloned.1.call-update) | async-done | bytes 6291472 | tf_op jit(solution)/shard_map/all_gather | solution.py:678
  74.4 5.0 %gather_fusion = bf16[256,768]{1,0:T(8,128)(2,1)S(1)} fusion(bf16[4096,768]{1,0:T(8,128)(2,1)} %all-gather.4.cloned.1.call-done.refs_4_, s32[1024]{0:T(1024)S(1)} %pad_clamp_fusion.1), kind=kCustom, calls=%fused_computation | custom fusion | bytes 787456 | tf_op jit(solution)/shard_map/jit(_take)/gather | solution.py:685
  79.4 1.1 convert_add_fusion.1.refs_0_
  80.5 10.5 %layer_forward.1 = bf16[256,768]{1,0:T(8,128)(2,1)} custom-call(f32[256,768]{1,0:T(8,128)} %convert_add_fusion.1.refs_0_, s32[256,1]{1,0:T(8,128)} %copy.47.refs_1_.refs_3_, s32[2,128]{1,0:T(2,128)} %refs_4_.11, bf16[1,768]{1,0:T(2,128)(2,1)} %refs_5_.7, bf16[1,768]{1,0:T(2,128)(2,1)} %refs_4_.7, bf16[1,2304]{1,0:T(2,128)(2,1)} %fusion.1.refs_5_, ...), custom_call_target="tpu_custom_call" | custom-call | tf_op jit(solution)/shard_map/layer_forward/pallas_call | solution.py:203
  91.0 3.6 collective-permute-start
  94.6 0.8 copy.48.refs_1_
  96.6 6.9 %collective-permute-done.refs_15_ = bf16[256,768]{1,0:T(8,128)(2,1)S(1)} collective-permute-done((bf16[256,768]{1,0:T(8,128)(2,1)}, bf16[256,768]{1,0:T(8,128)(2,1)S(1)}, u32[]{:S(2)}, u32[]{:S(2)}) %collective-permute-start) | collective-permute-done | bytes 393248 | tf_op jit(solution)/shard_map/ppermute | solution.py:711
  104.3 12.3 %layer_forward_save.1 = (f32[256,768]{1,0:T(8,128)}, f32[256,768]{1,0:T(8,128)}, bf16[256,2304]{1,0:T(8,128)(2,1)}, bf16[256,2304]{1,0:T(8,128)(2,1)}, f32[256,7...) custom-call(f32[256,768]{1,0:T(8,128)} %convert_add_fusion.1.refs_0_, s32[256,1]{1,0:T(8,128)} %copy.47.refs_1_.refs_3_, ...), custom_call_target="tpu_custom_call" | custom-call | tf_op jit(solution)/shard_map/layer_forward_save/pallas_call | solution.py:203
  116.5 13.0 %head.1 = (f32[256,768]{1,0:T(8,128)}, bf16[256,896]{1,0:T(8,128)(2,1)}, f32[1,768]{1,0:T(1,128)}, f32[1,768]{1,0:T(1,128)}, f32[1,1]{1,0:T(1,128)}) custom-call(f32[256,768]{1,0:T(8,128)} %get-tuple-element.53.refs_0_, s32[256,1]{1,0:T(8,128)} %copy.48.refs_1_, bf16[1,768]{1,0:T(2,128)(2,1)} %broadcast_in_dim.132.refs_2_, ...), custom_call_target="tpu_custom_call" | custom-call | tf_op jit(solution)/shard_map/head/pallas_call | solution.py:533
  129.6 1.0 slice.114
  130.6 1.3 collective-permute-start.3
  131.9 7.5 %collective-permute-done.3 = bf16[128,896]{1,0:T(8,128)(2,1)S(1)} collective-permute-done((bf16[128,896]{1,0:T(8,128)(2,1)S(1)}, bf16[128,896]{1,0:T(8,128)(2,1)S(1)}, u32[]{:S(2)}, u32[]{:S(2)}) %collective-permute-start.3) | collective-permute-done | bytes 229408 | tf_op jit(solution)/shard_map/ppermute | solution.py:719
  139.4 1.6 slice_select_fusion.1
  141.3 10.7 %mlp_back.1.refs_0_ = f32[256,768]{1,0:T(8,128)} custom-call(f32[256,768]{1,0:T(8,128)} %get-tuple-element.54.refs_0_, f32[256,768]{1,0:T(8,128)} %get-tuple-element.55.refs_1_, f32[256,3072]{1,0:T(8,128)} %get-tuple-element.56.refs_2_, bf16[1,768]{1,0:T(2,128)(2,1)} %refs_3_.7, bf16[1,768,3072]{2,1,0:T(8,128)(2,1)} %refs_4_.10, bf16[1,3072,768]{2,1,0:T(8,128)(2,1)} %refs_5_.6), custom_call_target="tpu_custom_call" | custom-call | tf_op jit(solution)/shard_map/mlp_back/pallas_call | solution.py:269
  152.1 12.1 %att_back.1 = bf16[256,768]{1,0:T(8,128)(2,1)} custom-call(f32[256,768]{1,0:T(8,128)} %mlp_back.1.refs_0_, f32[256,768]{1,0:T(8,128)} %get-tuple-element.57.refs_1_, bf16[256,2304]{1,0:T(8,128)(2,1)} %get-tuple-element.58.refs_2_, s32[256,1]{1,0:T(8,128)} %copy.47.refs_1_.refs_3_, s32[2,128]{1,0:T(2,128)} %refs_4_.11, bf16[1,768]{1,0:T(2,128)(2,1)} %refs_5_.7, ...), custom_call_target="tpu_custom_call" | custom-call | tf_op jit(solution)/shard_map/att_back/pallas_call | solution.py:364
  164.2 1.7 collective-permute-start.1
  166.0 0.8 select_convert_fusion.refs_8_
  166.8 8.9 %collective-permute-done.1 = bf16[256,768]{1,0:T(8,128)(2,1)S(1)} collective-permute-done((bf16[256,768]{1,0:T(8,128)(2,1)}, bf16[256,768]{1,0:T(8,128)(2,1)S(1)}, u32[]{:S(2)}, u32[]{:S(2)}) %collective-permute-start.1) | collective-permute-done | bytes 393248 | tf_op jit(solution)/shard_map/ppermute | solution.py:725
  175.7 0.8 convert_select_fusion.refs_6_.grads_ref
  176.5 11.0 %mlp_back_save.1 = (f32[256,768]{1,0:T(8,128)}, bf16[256,3072]{1,0:T(8,128)(2,1)}, f32[1,768]{1,0:T(1,128)}, f32[1,768]{1,0:T(1,128)}, f32[1,3072]{1,0:T(1,128)}, /*index=5*/f32[1,768]{1,0:T(1,128)}) custom-call(f32[256,768]{1,0:T(8,128)} %get-tuple-element.54.refs_0_, f32[256,768]{1,0:T(8,128)} %get-tuple-element.55.refs_1_, ...), custom_call_target="tpu_custom_call" | custom-call | tf_op jit(solution)/shard_map/mlp_back_save/pallas_call | solution.py:269
  187.6 12.1 %att_back_save.1 = (bf16[256,896]{1,0:T(8,128)(2,1)}, bf16[256,3072]{1,0:T(8,128)(2,1)}, f32[1,768]{1,0:T(1,128)}, f32[1,768]{1,0:T(1,128)}, f32[1,2304]{1,0:T(1,128)}, /*index=5*/f32[1,768]{1,0:T(1,128)}) custom-call(f32[256,768]{1,0:T(8,128)} %get-tuple-element.59.refs_0_, f32[256,768]{1,0:T(8,128)} %get-tuple-element.57.refs_1_, ...), custom_call_target="tpu_custom_call" | custom-call | tf_op jit(solution)/shard_map/att_back_save/pallas_call | solution.py:364
  199.7 1.0 slice.117
  200.7 1.9 collective-permute-start.5
  202.6 3.3 collective-permute-done.5
  205.9 1.7 slice_select_fusion
  208.2 3.1 shard_map.319
  211.8 2.0 collective-permute-done.16.theirs_ref
  213.8 2.8 collective-permute-done.17.other_ref
  217.4 3.5 shard_map.320
  221.5 2.7 shard_map.314
  224.7 1.8 collective-permute-done.7.theirs_ref
  226.5 0.8 copy-done.2
  227.3 4.1 shard_map.315
  231.4 1.5 collective-permute-start.9
  233.8 26.0 %collective-permute-done.18.rest_0_ = bf16[768,768]{1,0:T(8,128)(2,1)S(1)} collective-permute-done((bf16[768,768]{1,0:T(8,128)(2,1)}, bf16[768,768]{1,0:T(8,128)(2,1)S(1)}, u32[]{:S(2)}, u32[]{:S(2)}) %collective-permute-start.18) | collective-permute-done | bytes 1179680 | tf_op jit(solution)/shard_map/ppermute | solution.py:645
  259.8 1.0 copy-done.10
  260.8 3.9 shard_map.321
  264.7 1.5 collective-permute-start.19
  268.9 3.5 all-to-all-start
  273.1 11.7 %all-to-all-done = f32[16,1,673]{2,1,0:T(1,128)S(1)} async-done(((f32[16,1,673]{2,1,0:T(1,128)}), f32[16,1,673]{2,1,0:T(1,128)S(1)}, u32[]{:S(2)}, u32[]{:S(2)}) %all-to-all-start) | async-done | bytes 43104 | tf_op jit(solution)/shard_map/all_to_all | solution.py:780
  285.5 2.5 collective-permute-start.2
  288.6 4.2 %shard_map.317 = bf16[192,3072]{1,0:T(8,128)(2,1)} custom-call(bf16[1152,256]{1,0:T(8,128)(2,1)} %get-tuple-element.76.mine_ref, bf16[1152,256]{1,0:T(8,128)(2,1)} %copy-done.2, bf16[256,3072]{1,0:T(8,128)(2,1)} %get-tuple-element.81.grads_ref, bf16[256,3072]{1,0:T(8,128)(2,1)} %collective-permute-done.12.other_ref), custom_call_target="tpu_custom_call" | custom-call | tf_op jit(solution)/shard_map/pallas_call | solution.py:441
  294.7 2.0 collective-permute-start.20
  296.7 4.5 %shard_map.316 = (f32[96,3072]{1,0:T(8,128)}, bf16[96,3072]{1,0:T(8,128)(2,1)}) custom-call(bf16[1152,256]{1,0:T(8,128)(2,1)} %get-tuple-element.76.mine_ref, bf16[1152,256]{1,0:T(8,128)(2,1)} %copy-done.2, bf16[256,3072]{1,0:T(8,128)(2,1)} %get-tuple-element.78.grads_ref, bf16[256,3072]{1,0:T(8,128)(2,1)} %collective-permute-done.8.other_ref, ...), custom_call_target="tpu_custom_call" | custom-call | tf_op jit(solution)/shard_map/pallas_call | solution.py:441
  303.7 7.0 %collective-permute-done.20 = bf16[192,768]{1,0:T(8,128)(2,1)S(1)} collective-permute-done((bf16[192,768]{1,0:T(8,128)(2,1)}, bf16[192,768]{1,0:T(8,128)(2,1)S(1)}, u32[]{:S(2)}, u32[]{:S(2)}) %collective-permute-start.20) | collective-permute-done | bytes 294944 | tf_op jit(solution)/shard_map/ppermute | solution.py:645
  310.7 0.9 add_bitcast_fusion
  311.6 9.1 %collective-permute-done.13.rest_0_ = bf16[192,3072]{1,0:T(8,128)(2,1)S(1)} collective-permute-done((bf16[192,3072]{1,0:T(8,128)(2,1)}, bf16[192,3072]{1,0:T(8,128)(2,1)S(1)}, u32[]{:S(2)}, u32[]{:S(2)}) %collective-permute-start.13) | collective-permute-done | bytes 1179680 | tf_op jit(solution)/shard_map/ppermute | solution.py:645
  320.7 1.0 copy-done.14
  321.7 4.7 %shard_map.318 = (f32[96,3072]{1,0:T(8,128)}, bf16[96,3072]{1,0:T(8,128)(2,1)}) custom-call(bf16[1152,256]{1,0:T(8,128)(2,1)} %get-tuple-element.76.mine_ref, bf16[1152,256]{1,0:T(8,128)(2,1)} %copy-done.2, bf16[256,3072]{1,0:T(8,128)(2,1)} %get-tuple-element.81.grads_ref, bf16[256,3072]{1,0:T(8,128)(2,1)} %collective-permute-done.12.other_ref, ...), custom_call_target="tpu_custom_call" | custom-call | tf_op jit(solution)/shard_map/pallas_call | solution.py:441
  326.4 1.5 collective-permute-start.14
  328.0 1.1 collective-permute-start.11
  329.1 18.0 %collective-permute-done.14 = bf16[96,3072]{1,0:T(8,128)(2,1)S(1)} collective-permute-done((bf16[96,3072]{1,0:T(8,128)(2,1)}, bf16[96,3072]{1,0:T(8,128)(2,1)S(1)}, u32[]{:S(2)}, u32[]{:S(2)}) %collective-permute-start.14) | collective-permute-done | bytes 589856 | tf_op jit(solution)/shard_map/ppermute | solution.py:645
  348.2 13.0 %collective-permute-done.15 = bf16[48,3072]{1,0:T(8,128)(2,1)S(1)} collective-permute-done((bf16[48,3072]{1,0:T(8,128)(2,1)S(1)}, bf16[48,3072]{1,0:T(8,128)(2,1)S(1)}, u32[]{:S(2)}, u32[]{:S(2)}) %collective-permute-start.15) | collective-permute-done | bytes 294944 | tf_op jit(solution)/shard_map/ppermute | solution.py:645
  361.2 0.9 add_bitcast_fusion.1
  362.1 6.8 %table_head.1 = f32[256,768]{1,0:T(8,128)} custom-call(s32[1]{0:T(128)} %bitcast.11.refs_0_, bf16[2048,896]{1,0:T(8,128)(2,1)} %all-gather.6.cloned.1.call-done.refs_1_, bf16[256,768]{1,0:T(8,128)(2,1)} %refs_2_.5), custom_call_target="tpu_custom_call" | custom-call | tf_op jit(solution)/shard_map/table_head/pallas_call | solution.py:579
  369.5 5.5 %lookup_back.1 = (f32[256,768]{1,0:T(8,128)}, f32[64,768]{1,0:T(8,128)}) custom-call(s32[2]{0:T(128)} %pad_add_fusion.base_ref, bf16[2048,896]{1,0:T(8,128)(2,1)} %all-gather.8.cloned.1.call-done.ext_ref), custom_call_target="tpu_custom_call" | custom-call | tf_op jit(solution)/shard_map/lookup_back/pallas_call | solution.py:621
  375.0 1.4 fusion
  376.3 1.5 collective-permute-start.6
  377.8 0.8 slice_bitcast_fusion
  378.6 20.5 %collective-permute-done.6 = bf16[320,768]{1,0:T(8,128)(2,1)S(1)} collective-permute-done((bf16[320,768]{1,0:T(8,128)(2,1)S(1)}, bf16[320,768]{1,0:T(8,128)(2,1)S(1)}, u32[]{:S(2)}, u32[]{:S(2)}) %collective-permute-start.6) | collective-permute-done | bytes 491552 | tf_op jit(solution)/shard_map/ppermute | solution.py:795
  399.9 1.0 slice_add_fusion
  (145 shorter events, 17.7 us)
Async XLA Ops:
  7.2 3.2 copy-start
  7.2 67.2 %all-gather.4.cloned.1.call-start = ((), (), s32[]{:S(2)}) async-start(), calls=%async_computation.1 | async-start | bytes 6684672 | tf_op jit(solution)/shard_map/all_gather | solution.py:678
  7.9 354.2 %all-gather.6.cloned.1.call-start = ((), (), s32[]{:S(2)}) async-start(), calls=%async_computation.2 | async-start | bytes 3899392 | tf_op jit(solution)/shard_map/all_gather | solution.py:721
  10.4 1.2 copy-start.18
  10.5 1.3 copy-start.19
  80.5 14.1 %copy-start.31 = (s32[2,128]{1,0:T(2,128)S(1)}, s32[2,128]{1,0:T(2,128)}, u32[]{:S(2)}) copy-start(s32[2,128]{1,0:T(2,128)} %param.20) | copy-start | bytes 3076
  80.5 14.9 %copy-start.29 = (bf16[768]{0:T(1024)(128)(2,1)S(1)}, bf16[768]{0:T(1024)(128)(2,1)}, u32[]{:S(2)}) copy-start(bf16[768]{0:T(1024)(128)(2,1)} %param.24) | copy-start | bytes 4612
  80.5 15.5 %copy-start.30 = (bf16[768]{0:T(1024)(128)(2,1)S(1)}, bf16[768]{0:T(1024)(128)(2,1)}, u32[]{:S(2)}) copy-start(bf16[768]{0:T(1024)(128)(2,1)} %param.25) | copy-start | bytes 4612
  91.0 12.5 %collective-permute-start = (bf16[256,768]{1,0:T(8,128)(2,1)}, bf16[256,768]{1,0:T(8,128)(2,1)S(1)}, u32[]{:S(2)}, u32[]{:S(2)}) collective-permute-start(bf16[256,768]{1,0:T(8,128)(2,1)} %layer_forward.1), channel_id=1, source_target_pairs={{0,16},{1,17},{2,18},{3,19},{4,20},{5,21},{6,22},{7,23},{8,24},{9,... | collective-permute-start | bytes 1179656 | tf_op jit(solution)/shard_map/ppermute | solution.py:711
  103.5 0.7 copy-start.16
  130.6 8.8 %collective-permute-start.3 = (bf16[128,896]{1,0:T(8,128)(2,1)S(1)}, bf16[128,896]{1,0:T(8,128)(2,1)S(1)}, u32[]{:S(2)}, u32[]{:S(2)}) collective-permute-start(bf16[128,896]{1,0:T(8,128)(2,1)S(1)} %slice.114), channel_id=1, source_target_pairs={{16,0},{17,1},{18,2},{19,3},{20,4},{21,5},{22,6},{23,7},{24,8},{25... | collective-permute-start | bytes 688136 | tf_op jit(solution)/shard_map/ppermute | solution.py:719
  141.0 228.5 %all-gather.8.cloned.1.call-start = ((), (), s32[]{:S(2)}) async-start(), calls=%async_computation.3 | async-start | bytes 3899392 | tf_op jit(solution)/shard_map/all_gather | solution.py:766
  152.1 23.7 %copy-start.3 = (f32[256,768]{1,0:T(8,128)S(1)}, f32[256,768]{1,0:T(8,128)}, u32[]{:S(2)}) copy-start(f32[256,768]{1,0:T(8,128)} %get-tuple-element.54.refs_0_) | copy-start | bytes 2359300
  164.2 11.5 %collective-permute-start.1 = (bf16[256,768]{1,0:T(8,128)(2,1)}, bf16[256,768]{1,0:T(8,128)(2,1)S(1)}, u32[]{:S(2)}, u32[]{:S(2)}) collective-permute-start(bf16[256,768]{1,0:T(8,128)(2,1)} %att_back.1), channel_id=1, source_target_pairs={{16,0},{17,1},{18,2},{19,3},{20,4},{21,5},{22,6},{23,7},{24,8},{25... | collective-permute-start | bytes 1179656 | tf_op jit(solution)/shard_map/ppermute | solution.py:725
  200.7 11.2 %copy-start.5 = (bf16[256,768]{1,0:T(8,128)(2,1)S(1)}, bf16[256,768]{1,0:T(8,128)(2,1)}, u32[]{:S(2)}) copy-start(bf16[256,768]{1,0:T(8,128)(2,1)} %convert_select_fusion.refs_6_.grads_ref) | copy-start | bytes 1179652
  200.7 5.2 %collective-permute-start.5 = (bf16[128,896]{1,0:T(8,128)(2,1)S(1)}, bf16[128,896]{1,0:T(8,128)(2,1)S(1)}, u32[]{:S(2)}, u32[]{:S(2)}) collective-permute-start(bf16[128,896]{1,0:T(8,128)(2,1)S(1)} %slice.117), channel_id=1, source_target_pairs={{0,16},{1,17},{2,18},{3,19},{4,20},{5,21},{6,22},{7,23},{8,24},{9,... | collective-permute-start | bytes 688136 | tf_op jit(solution)/shard_map/ppermute | solution.py:764
  211.3 2.5 collective-permute-start.16
  211.3 15.2 %collective-permute-start.8 = (bf16[256,3072]{1,0:T(8,128)(2,1)}, bf16[256,3072]{1,0:T(8,128)(2,1)}, u32[]{:S(2)}, u32[]{:S(2)}) collective-permute-start(bf16[256,3072]{1,0:T(8,128)(2,1)} %get-tuple-element.78.grads_ref), channel_id=1, source_target_pairs={{0,1},{1,0},{2,3},{3,2},{4,5},{5,4},{6,7},{7,6},{8,9},{9,8},{10,11... | collective-permute-start | bytes 4718600 | tf_op jit(solution)/shard_map/ppermute | solution.py:645
  211.8 4.8 %collective-permute-start.17 = (bf16[256,768]{1,0:T(8,128)(2,1)S(1)}, bf16[256,768]{1,0:T(8,128)(2,1)S(1)}, u32[]{:S(2)}, u32[]{:S(2)}) collective-permute-start(bf16[256,768]{1,0:T(8,128)(2,1)S(1)} %copy-done.5), channel_id=1, source_target_pairs={{0,1},{1,0},{2,3},{3,2},{4,5},{5,4},{6,7},{7,6},{8,9},{9,8},{10,11... | collective-permute-start | bytes 1179656 | tf_op jit(solution)/shard_map/ppermute | solution.py:645
  213.8 2.8 copy-start.6
  216.6 0.8 copy-start.9
  217.4 4.1 copy-start.4
  220.9 38.9 %collective-permute-start.18 = (bf16[768,768]{1,0:T(8,128)(2,1)}, bf16[768,768]{1,0:T(8,128)(2,1)S(1)}, u32[]{:S(2)}, u32[]{:S(2)}) collective-permute-start(bf16[768,768]{1,0:T(8,128)(2,1)} %shard_map.320), channel_id=1, source_target_pairs={{0,2},{1,3},{2,0},{3,1},{4,6},{5,7},{6,4},{7,5},{8,10},{9,11},{10,... | collective-permute-start | bytes 3538952 | tf_op jit(solution)/shard_map/ppermute | solution.py:645
  221.5 67.2 %collective-permute-start.12 = (bf16[256,3072]{1,0:T(8,128)(2,1)S(1)}, bf16[256,3072]{1,0:T(8,128)(2,1)}, u32[]{:S(2)}, u32[]{:S(2)}) collective-permute-start(bf16[256,3072]{1,0:T(8,128)(2,1)S(1)} %copy-done.4), channel_id=1, source_target_pairs={{0,1},{1,0},{2,3},{3,2},{4,5},{5,4},{6,7},{7,6},{8,9},{9,8},{10,11... | collective-permute-start | bytes 4718600 | tf_op jit(solution)/shard_map/ppermute | solution.py:645
  224.2 2.4 collective-permute-start.7
  226.5 0.8 copy-start.2
  227.3 5.5 %copy-start.22 = (f32[1,768]{1,0:T(1,128)S(1)}, f32[1,768]{1,0:T(1,128)}, u32[]{:S(2)}) copy-start(f32[1,768]{1,0:T(1,128)} %get-tuple-element.68) | copy-start | bytes 9220
  227.3 5.6 %copy-start.21 = (f32[1,768]{1,0:T(1,128)S(1)}, f32[1,768]{1,0:T(1,128)}, u32[]{:S(2)}) copy-start(f32[1,768]{1,0:T(1,128)} %get-tuple-element.69) | copy-start | bytes 9220
  231.4 65.3 %collective-permute-start.9 = (bf16[192,3072]{1,0:T(8,128)(2,1)}, bf16[192,3072]{1,0:T(8,128)(2,1)}, u32[]{:S(2)}, u32[]{:S(2)}) collective-permute-start(bf16[192,3072]{1,0:T(8,128)(2,1)} %shard_map.315), channel_id=1, source_target_pairs={{0,2},{1,3},{2,0},{3,1},{4,6},{5,7},{6,4},{7,5},{8,10},{9,11},{10,... | collective-permute-start | bytes 3538952 | tf_op jit(solution)/shard_map/ppermute | solution.py:645
  233.7 32.5 %copy-start.20 = (f32[1,2304]{1,0:T(1,128)S(1)}, f32[1,2304]{1,0:T(1,128)}, u32[]{:S(2)}) copy-start(f32[1,2304]{1,0:T(1,128)} %get-tuple-element.62) | copy-start | bytes 27652
  233.7 32.5 %copy-start.28 = (f32[1,768]{1,0:T(1,128)S(1)}, f32[1,768]{1,0:T(1,128)}, u32[]{:S(2)}) copy-start(f32[1,768]{1,0:T(1,128)} %get-tuple-element.60) | copy-start | bytes 9220
  233.7 32.6 %copy-start.27 = (f32[1,768]{1,0:T(1,128)S(1)}, f32[1,768]{1,0:T(1,128)}, u32[]{:S(2)}) copy-start(f32[1,768]{1,0:T(1,128)} %get-tuple-element.61) | copy-start | bytes 9220
  233.7 32.8 %copy-start.26 = (f32[1,768]{1,0:T(1,128)S(1)}, f32[1,768]{1,0:T(1,128)}, u32[]{:S(2)}) copy-start(f32[1,768]{1,0:T(1,128)} %get-tuple-element.63) | copy-start | bytes 9220
  233.8 32.9 %copy-start.25 = (f32[1,768]{1,0:T(1,128)S(1)}, f32[1,768]{1,0:T(1,128)}, u32[]{:S(2)}) copy-start(f32[1,768]{1,0:T(1,128)} %get-tuple-element.64) | copy-start | bytes 9220
  233.8 33.0 %copy-start.24 = (f32[1,768]{1,0:T(1,128)S(1)}, f32[1,768]{1,0:T(1,128)}, u32[]{:S(2)}) copy-start(f32[1,768]{1,0:T(1,128)} %get-tuple-element.65) | copy-start | bytes 9220
  233.8 33.6 %copy-start.17 = (f32[1,3072]{1,0:T(1,128)S(1)}, f32[1,3072]{1,0:T(1,128)}, u32[]{:S(2)}) copy-start(f32[1,3072]{1,0:T(1,128)} %get-tuple-element.66) | copy-start | bytes 36868
  233.8 34.3 %copy-start.23 = (f32[1,768]{1,0:T(1,128)S(1)}, f32[1,768]{1,0:T(1,128)}, u32[]{:S(2)}) copy-start(f32[1,768]{1,0:T(1,128)} %get-tuple-element.67) | copy-start | bytes 9220
  259.8 1.0 copy-start.10
  264.7 29.3 %collective-permute-start.19 = (bf16[384,768]{1,0:T(8,128)(2,1)}, bf16[384,768]{1,0:T(8,128)(2,1)S(1)}, u32[]{:S(2)}, u32[]{:S(2)}) collective-permute-start(bf16[384,768]{1,0:T(8,128)(2,1)} %get-tuple-element.88), channel_id=1, source_target_pairs={{0,4},{1,5},{2,6},{3,7},{4,0},{5,1},{6,2},{7,3},{8,12},{9,13},{10,... | collective-permute-start | bytes 1769480 | tf_op jit(solution)/shard_map/ppermute | solution.py:645
  268.9 15.8 %all-to-all-start = ((f32[16,1,673]{2,1,0:T(1,128)}), f32[16,1,673]{2,1,0:T(1,128)S(1)}, u32[]{:S(2)}, u32[]{:S(2)}) async-start(f32[16,1,673]{2,1,0:T(1,128)} %all_to_all.6), calls=%async_computation | async-start | bytes 98304 | tf_op jit(solution)/shard_map/all_to_all | solution.py:780
  285.5 16.3 %collective-permute-start.2 = (f32[97]{0:T(128)S(1)}, f32[97]{0:T(128)S(1)}, u32[]{:S(2)}, u32[]{:S(2)}) collective-permute-start(f32[97]{0:T(128)S(1)} %slice.112), channel_id=1, source_target_pairs={{0,16},{16,0},{1,17},{17,1},{2,18},{18,2},{3,19},{19,3},{4,20},{20... | collective-permute-start | bytes 1172 | tf_op jit(solution)/shard_map/ppermute | solution.py:789
  288.6 5.3 %copy-start.11 = (f32[384,768]{1,0:T(8,128)S(1)}, f32[384,768]{1,0:T(8,128)}, u32[]{:S(2)}) copy-start(f32[384,768]{1,0:T(8,128)} %get-tuple-element.87) | copy-start | bytes 3538948
  292.8 27.9 %collective-permute-start.13 = (bf16[192,3072]{1,0:T(8,128)(2,1)}, bf16[192,3072]{1,0:T(8,128)(2,1)S(1)}, u32[]{:S(2)}, u32[]{:S(2)}) collective-permute-start(bf16[192,3072]{1,0:T(8,128)(2,1)} %shard_map.317), channel_id=1, source_target_pairs={{0,2},{1,3},{2,0},{3,1},{4,6},{5,7},{6,4},{7,5},{8,10},{9,11},{10,... | collective-permute-start | bytes 3538952 | tf_op jit(solution)/shard_map/ppermute | solution.py:645
  294.7 16.0 %collective-permute-start.20 = (bf16[192,768]{1,0:T(8,128)(2,1)}, bf16[192,768]{1,0:T(8,128)(2,1)S(1)}, u32[]{:S(2)}, u32[]{:S(2)}) collective-permute-start(bf16[192,768]{1,0:T(8,128)(2,1)} %add_convert_fusion), channel_id=1, source_target_pairs={{0,8},{1,9},{2,10},{3,11},{4,12},{5,13},{6,14},{7,15},{8,0},{9,1},... | collective-permute-start | bytes 884744 | tf_op jit(solution)/shard_map/ppermute | solution.py:645
  301.2 26.7 %collective-permute-start.10 = (bf16[96,3072]{1,0:T(8,128)(2,1)}, bf16[96,3072]{1,0:T(8,128)(2,1)S(1)}, u32[]{:S(2)}, u32[]{:S(2)}) collective-permute-start(bf16[96,3072]{1,0:T(8,128)(2,1)} %get-tuple-element.80), channel_id=1, source_target_pairs={{0,4},{1,5},{2,6},{3,7},{4,0},{5,1},{6,2},{7,3},{8,12},{9,13},{10,... | collective-permute-start | bytes 1769480 | tf_op jit(solution)/shard_map/ppermute | solution.py:645
  311.6 16.3 %copy-start.12 = (f32[96,3072]{1,0:T(8,128)S(1)}, f32[96,3072]{1,0:T(8,128)}, u32[]{:S(2)}) copy-start(f32[96,3072]{1,0:T(8,128)} %get-tuple-element.79) | copy-start | bytes 3538948
  320.7 1.0 copy-start.14
  326.4 20.8 %copy-start.13 = (f32[96,3072]{1,0:T(8,128)S(1)}, f32[96,3072]{1,0:T(8,128)}, u32[]{:S(2)}) copy-start(f32[96,3072]{1,0:T(8,128)} %get-tuple-element.82) | copy-start | bytes 3538948
  326.4 20.7 %collective-permute-start.14 = (bf16[96,3072]{1,0:T(8,128)(2,1)}, bf16[96,3072]{1,0:T(8,128)(2,1)S(1)}, u32[]{:S(2)}, u32[]{:S(2)}) collective-permute-start(bf16[96,3072]{1,0:T(8,128)(2,1)} %get-tuple-element.83), channel_id=1, source_target_pairs={{0,4},{1,5},{2,6},{3,7},{4,0},{5,1},{6,2},{7,3},{8,12},{9,13},{10,... | collective-permute-start | bytes 1769480 | tf_op jit(solution)/shard_map/ppermute | solution.py:645
  328.0 19.5 %collective-permute-start.11 = (bf16[48,3072]{1,0:T(8,128)(2,1)S(1)}, bf16[48,3072]{1,0:T(8,128)(2,1)S(1)}, u32[]{:S(2)}, u32[]{:S(2)}) collective-permute-start(bf16[48,3072]{1,0:T(8,128)(2,1)S(1)} %add_convert_fusion.2), channel_id=1, source_target_pairs={{0,8},{1,9},{2,10},{3,11},{4,12},{5,13},{6,14},{7,15},{8,0},{9,1},... | collective-permute-start | bytes 884744 | tf_op jit(solution)/shard_map/ppermute | solution.py:645
  347.2 14.0 %collective-permute-start.15 = (bf16[48,3072]{1,0:T(8,128)(2,1)S(1)}, bf16[48,3072]{1,0:T(8,128)(2,1)S(1)}, u32[]{:S(2)}, u32[]{:S(2)}) collective-permute-start(bf16[48,3072]{1,0:T(8,128)(2,1)S(1)} %add_convert_fusion.1), channel_id=1, source_target_pairs={{0,8},{1,9},{2,10},{3,11},{4,12},{5,13},{6,14},{7,15},{8,0},{9,1},... | collective-permute-start | bytes 884744 | tf_op jit(solution)/shard_map/ppermute | solution.py:645
  368.9 31.0 %collective-permute-start.4 = (f32[256,768]{1,0:T(8,128)}, f32[256,768]{1,0:T(8,128)S(1)}, u32[]{:S(2)}, u32[]{:S(2)}) collective-permute-start(f32[256,768]{1,0:T(8,128)} %table_head.1), channel_id=1, source_target_pairs={{0,16},{16,0},{1,17},{17,1},{2,18},{18,2},{3,19},{19,3},{4,20},{20... | collective-permute-start | bytes 2359304 | tf_op jit(solution)/shard_map/ppermute | solution.py:792
  375.0 24.2 %copy-start.8 = (f32[256,768]{1,0:T(8,128)S(1)}, f32[256,768]{1,0:T(8,128)}, u32[]{:S(2)}) copy-start(f32[256,768]{1,0:T(8,128)} %get-tuple-element.73) | copy-start | bytes 2359300
  375.0 24.2 %copy-start.15 = (f32[64,768]{1,0:T(8,128)S(1)}, f32[64,768]{1,0:T(8,128)}, u32[]{:S(2)}) copy-start(f32[64,768]{1,0:T(8,128)} %get-tuple-element.74) | copy-start | bytes 589828
  376.3 22.8 %collective-permute-start.6 = (bf16[320,768]{1,0:T(8,128)(2,1)S(1)}, bf16[320,768]{1,0:T(8,128)(2,1)S(1)}, u32[]{:S(2)}, u32[]{:S(2)}) collective-permute-start(bf16[320,768]{1,0:T(8,128)(2,1)S(1)} %fusion), channel_id=1, source_target_pairs={{0,16},{16,0},{1,17},{17,1},{2,18},{18,2},{3,19},{19,3},{4,20},{20... | collective-permute-start | bytes 1474568 | tf_op jit(solution)/shard_map/ppermute | solution.py:795
  378.6 21.3 %copy-start.7 = (f32[256,768]{1,0:T(8,128)S(1)}, f32[256,768]{1,0:T(8,128)}, u32[]{:S(2)}) copy-start(f32[256,768]{1,0:T(8,128)} %table_head.1) | copy-start | bytes 2359300
  399.2 1.7 copy-start.1
Sparse Core Ops, SparseCore 0:
  10.3 64.1 all-gather.3
  141.1 45.4 all-gather.5
  207.7 57.6 all-gather.7
where the time goes:
time: 416 us; the launch traced here: 409 us
  waiting for transfers between devices  201 us (48%)
  Pallas kernels  125 us (30%)
  starting transfers between devices  27.5 us (7%)
  local copies, waits for them, and re-layouts  23.9 us (6%)
  between operations  16.9 us (4%)
  other arithmetic  14.4 us (3%)
    ppermute x14, waiting for transfers between devices, swap(): return lax.ppermute(array, 'dp', [(i, i ^ bit) for i in range(self.size)])  79.7 us
    all_gather x1, waiting for transfers between devices, body(): full_table = lax.all_gather(token_embed, 'dp', axis=0, tiled=True)  62.1 us
    pallas_call x6, Pallas kernels, product(): pl.pallas_call(kernel, out_shape=outs, in_specs=[vmem_spec()] * (4 + len(...  24.8 us
    pallas_call x2, Pallas kernels, att_back(): pl.pallas_call(kernel, out_shape=outs, in_specs=[vmem_spec()] * 6 + [any_...  24.3 us
    pallas_call x2, Pallas kernels, forward_layer(): pl.pallas_call(kernel, out_shape=outs, in_specs=[vmem_spec()] * 11 + [any...  22.8 us
    pallas_call x2, Pallas kernels, mlp_back(): pl.pallas_call(kernel, out_shape=outs, in_specs=[vmem_spec()] * 4 + [any_...  21.8 us
    ppermute x1, waiting for transfers between devices, body(): late = late + lax.ppermute(late.astype(BF), 'section', both).astype(F32)  20.5 us
    pallas_call x1, Pallas kernels, head(): pl.pallas_call(kernel, grid=(2, blocks), out_shape=outs, in_specs=[full((...  13 us
  transfers between devices with their start and end apart: 25, of which 15 were waited for; matrix products, arithmetic and copies ran while one was open for 6% of the time, Pallas kernels for 22%

commit v1 on v0

--- a/solution.py
+++ b/solution.py
@@ -207,7 +207,7 @@
         out_specs=[vmem_spec()] * len(outs),
         scratch_shapes=scratch,
         compiler_params=params(),
-        name="layer_forward_save" if save else "layer_forward",
+        name="fwd2" if save else "fwd1",
     )(hidden, seg_col, seg_row, *vectors, *weights, *extra)
 
 
@@ -216,9 +216,14 @@
         gy_ref, first, dx1_ref, gin_ref, dg2, db2, dfc, dproj, wfc, wproj, sems = rest
     else:
         dx1_ref, wfc, wproj, sems = rest
-    copies = start_copies(((wproj_h.at[0], wproj), (wfc_h.at[0], wfc)), sems)
     width = dy_ref.shape[1]
     units = inner_ref.shape[1]
+    pieces = []
+    for low in range(0, units, width):
+        these = slice(low, low + width)
+        pieces += [(wproj_h.at[0, these, :], wproj.at[these, :])]
+        pieces += [(wfc_h.at[0, :, these], wfc.at[:, these])]
+    copies = start_copies(pieces, sems)
     dy = dy_ref[...]
     if save:
         gy = gy_ref[...]
@@ -227,11 +232,10 @@
     else:
         gy = dy.astype(BF)
     hat, scale = normalised(x1_ref[...])
-    copies[0].wait()
-    copies[1].wait()
     da2 = jnp.zeros(dy.shape, F32)
     for part in range(units // width):
         cols = slice(part * width, (part + 1) * width)
+        copies[2 * part].wait()
         dact = nt(gy, wproj[cols, :])
         inner = inner_ref[:, cols]
         half, bend, square = gelu_parts(inner)
@@ -242,6 +246,7 @@
         if save:
             gin_ref[:, cols] = gin
             dfc[:, cols] = rowsum(gin.astype(F32))
+        copies[2 * part + 1].wait()
         da2 = da2 + nt(gin, wfc[:, cols])
     if save:
         dg2[...] = rowsum(da2 * hat)
@@ -273,10 +278,10 @@
         out_specs=[vmem_spec()] * len(outs),
         scratch_shapes=[
             pltpu.VMEM(wfc.shape[1:], BF), pltpu.VMEM(wproj.shape[1:], BF),
-            pltpu.SemaphoreType.DMA((2,)),
+            pltpu.SemaphoreType.DMA((2 * (units // width),)),
         ],
         compiler_params=params(),
-        name="mlp_back_save" if save else "mlp_back",
+        name="mlp2" if save else "mlp1",
     )(dy, x1, inner, gain, wfc, wproj, *extra)
 
 
@@ -368,7 +373,7 @@
         out_specs=[vmem_spec()] * len(outs),
         scratch_shapes=scratch,
         compiler_params=params(),
-        name="att_back_save" if save else "att_back",
+        name="att2" if save else "att1",
     )(dx1, hidden, qkv, seg_col, seg_row, gain, wqkv, wo, *extra)
 
 
@@ -587,7 +592,7 @@
         ],
         out_specs=pl.BlockSpec(shard.shape, lambda r: (0, 0)),
         compiler_params=params(),
-        name="table_head",
+        name="thead",
     )(base, ext, shard)
 
 
@@ -628,7 +633,7 @@
         ],
         out_specs=[pl.BlockSpec(out.shape, lambda r: (0, 0)) for out in outs],
         compiler_params=params(),
-        name="lookup_back",
+        name="look",
     )(bases, ext)
 
 
@@ -646,7 +651,9 @@
 
     def order(self):
         bits = self.line.bit_length() - 1
-        turned = [int(format(k, "b").zfill(bits)[::-1], 2) if bits else 0 for k in range(self.line)]
+        turned = [
+            sum(((k >> i) & 1) << (bits - 1 - i) for i in range(bits)) for k in range(self.line)
+        ]
         return [self.place ^ k for k in turned]
 
     def line_sum(self, kept, sent):

time: 416 us -> 415 us (level)
  transfers between devices with their start and end apart: 25 -> 25, of which waited for: 15 -> 15; matrix products, arithmetic and copies ran while one was open for 6% -> 6% of each run, Pallas kernels for 22% -> 21%
where the time goes in v1:
time: 415 us; the launch traced here: 407 us
  waiting for transfers between devices  202 us (49%)
  Pallas kernels  123 us (30%)
  starting transfers between devices  27.6 us (7%)
  local copies, waits for them, and re-layouts  23.9 us (6%)
  between operations  16.9 us (4%)
  other arithmetic  14.4 us (3%)
    ppermute x14, waiting for transfers between devices, swap(): return lax.ppermute(array, 'dp', [(i, i ^ bit) for i in range(self.size)])  79.6 us
    all_gather x1, waiting for transfers between devices, body(): full_table = lax.all_gather(token_embed, 'dp', axis=0, tiled=True)  62.1 us
    pallas_call x6, Pallas kernels, product(): pl.pallas_call(kernel, out_shape=outs, in_specs=[vmem_spec()] * (4 + len(...  24.8 us
    pallas_call x2, Pallas kernels, att_back(): pl.pallas_call(kernel, out_shape=outs, in_specs=[vmem_spec()] * 6 + [any_...  24.2 us
    pallas_call x2, Pallas kernels, forward_layer(): pl.pallas_call(kernel, out_shape=outs, in_specs=[vmem_spec()] * 11 + [any...  22.8 us
    ppermute x1, waiting for transfers between devices, body(): late = late + lax.ppermute(late.astype(BF), 'section', both).astype(F32)  20.5 us
    pallas_call x2, Pallas kernels, mlp_back(): pl.pallas_call(kernel, out_shape=outs, in_specs=[vmem_spec()] * 4 + [any_...  19.8 us
    pallas_call x1, Pallas kernels, head(): pl.pallas_call(kernel, grid=(2, blocks), out_shape=outs, in_specs=[full((...  13 us
  transfers between devices with their start and end apart: 25, of which 15 were waited for; matrix products, arithmetic and copies ran while one was open for 6% of the time, Pallas kernels for 21%

profile of v1, /device:TPU:0, one launch (start us, length us, event | category | flops | bytes accessed | tf_op | source)
XLA Modules:
  0.0 407.0 jit_solution(17107418690034477021)
XLA Ops:
  8.0 1.5 copy.47.refs_1_.refs_3_
  9.5 0.9 convert_reduce_fusion
  10.5 1.2 gather_fusion.1
  12.4 62.1 %all-gather.4.cloned.1.call-done.refs_4_ = bf16[4096,768]{1,0:T(8,128)(2,1)} async-done(((bf16[256,768]{1,0:T(8,128)(2,1)}), bf16[4096,768]{1,0:T(8,128)(2,1)}) %all-gather.4.cloned.1.call-update) | async-done | bytes 6291472 | tf_op jit(solution)/shard_map/all_gather | solution.py:685
  74.4 5.0 %gather_fusion = bf16[256,768]{1,0:T(8,128)(2,1)S(1)} fusion(bf16[4096,768]{1,0:T(8,128)(2,1)} %all-gather.4.cloned.1.call-done.refs_4_, s32[1024]{0:T(1024)S(1)} %pad_clamp_fusion.1), kind=kCustom, calls=%fused_computation | custom fusion | bytes 787456 | tf_op jit(solution)/shard_map/jit(_take)/gather | solution.py:692
  79.4 1.1 convert_add_fusion.1.refs_0_
  80.5 10.5 %fwd1.1 = bf16[256,768]{1,0:T(8,128)(2,1)} custom-call(f32[256,768]{1,0:T(8,128)} %convert_add_fusion.1.refs_0_, s32[256,1]{1,0:T(8,128)} %copy.47.refs_1_.refs_3_, s32[2,128]{1,0:T(2,128)} %refs_4_.11, bf16[1,768]{1,0:T(2,128)(2,1)} %refs_5_.7, bf16[1,768]{1,0:T(2,128)(2,1)} %refs_4_.7, bf16[1,2304]{1,0:T(2,128)(2,1)} %fusion.1.refs_5_, ...), custom_call_target="tpu_custom_call" | custom-call | tf_op jit(solution)/shard_map/fwd1/pallas_call | solution.py:203
  91.0 3.6 collective-permute-start
  94.6 0.8 copy.48.refs_1_
  96.6 6.9 %collective-permute-done.refs_15_ = bf16[256,768]{1,0:T(8,128)(2,1)S(1)} collective-permute-done((bf16[256,768]{1,0:T(8,128)(2,1)}, bf16[256,768]{1,0:T(8,128)(2,1)S(1)}, u32[]{:S(2)}, u32[]{:S(2)}) %collective-permute-start) | collective-permute-done | bytes 393248 | tf_op jit(solution)/shard_map/ppermute | solution.py:718
  104.3 12.3 %fwd2.1 = (f32[256,768]{1,0:T(8,128)}, f32[256,768]{1,0:T(8,128)}, bf16[256,2304]{1,0:T(8,128)(2,1)}, bf16[256,2304]{1,0:T(8,128)(2,1)}, f32[256,768]{1,0:T(8,12...) custom-call(f32[256,768]{1,0:T(8,128)} %convert_add_fusion.1.refs_0_, s32[256,1]{1,0:T(8,128)} %copy.47.refs_1_.refs_3_, ...), custom_call_target="tpu_custom_call" | custom-call | tf_op jit(solution)/shard_map/fwd2/pallas_call | solution.py:203
  116.5 13.0 %head.1 = (f32[256,768]{1,0:T(8,128)}, bf16[256,896]{1,0:T(8,128)(2,1)}, f32[1,768]{1,0:T(1,128)}, f32[1,768]{1,0:T(1,128)}, f32[1,1]{1,0:T(1,128)}) custom-call(f32[256,768]{1,0:T(8,128)} %get-tuple-element.53.refs_0_, s32[256,1]{1,0:T(8,128)} %copy.48.refs_1_, bf16[1,768]{1,0:T(2,128)(2,1)} %broadcast_in_dim.132.refs_2_, ...), custom_call_target="tpu_custom_call" | custom-call | tf_op jit(solution)/shard_map/head/pallas_call | solution.py:538
  129.6 1.0 slice.114
  130.6 1.3 collective-permute-start.3
  131.9 7.5 %collective-permute-done.3 = bf16[128,896]{1,0:T(8,128)(2,1)S(1)} collective-permute-done((bf16[128,896]{1,0:T(8,128)(2,1)S(1)}, bf16[128,896]{1,0:T(8,128)(2,1)S(1)}, u32[]{:S(2)}, u32[]{:S(2)}) %collective-permute-start.3) | collective-permute-done | bytes 229408 | tf_op jit(solution)/shard_map/ppermute | solution.py:726
  139.4 1.6 slice_select_fusion.1
  141.3 9.7 %mlp1.1.refs_0_ = f32[256,768]{1,0:T(8,128)} custom-call(f32[256,768]{1,0:T(8,128)} %get-tuple-element.54.refs_0_, f32[256,768]{1,0:T(8,128)} %get-tuple-element.55.refs_1_, f32[256,3072]{1,0:T(8,128)} %get-tuple-element.56.refs_2_, bf16[1,768]{1,0:T(2,128)(2,1)} %refs_3_.7, bf16[1,768,3072]{2,1,0:T(8,128)(2,1)} %refs_4_.10, bf16[1,3072,768]{2,1,0:T(8,128)(2,1)} %refs_5_.6), custom_call_target="tpu_custom_call" | custom-call | tf_op jit(solution)/shard_map/mlp1/pallas_call | solution.py:274
  151.0 12.1 %att1.1 = bf16[256,768]{1,0:T(8,128)(2,1)} custom-call(f32[256,768]{1,0:T(8,128)} %mlp1.1.refs_0_, f32[256,768]{1,0:T(8,128)} %get-tuple-element.57.refs_1_, bf16[256,2304]{1,0:T(8,128)(2,1)} %get-tuple-element.58.refs_2_, s32[256,1]{1,0:T(8,128)} %copy.47.refs_1_.refs_3_, s32[2,128]{1,0:T(2,128)} %refs_4_.11, bf16[1,768]{1,0:T(2,128)(2,1)} %refs_5_.7, ...), custom_call_target="tpu_custom_call" | custom-call | tf_op jit(solution)/shard_map/att1/pallas_call | solution.py:369
  163.1 1.7 collective-permute-start.1
  164.9 0.8 select_convert_fusion.refs_8_
  165.7 9.1 %collective-permute-done.1 = bf16[256,768]{1,0:T(8,128)(2,1)S(1)} collective-permute-done((bf16[256,768]{1,0:T(8,128)(2,1)}, bf16[256,768]{1,0:T(8,128)(2,1)S(1)}, u32[]{:S(2)}, u32[]{:S(2)}) %collective-permute-start.1) | collective-permute-done | bytes 393248 | tf_op jit(solution)/shard_map/ppermute | solution.py:732
  174.8 0.8 convert_select_fusion.refs_6_.grads_ref
  175.6 10.1 %mlp2.1 = (f32[256,768]{1,0:T(8,128)}, bf16[256,3072]{1,0:T(8,128)(2,1)}, f32[1,768]{1,0:T(1,128)}, f32[1,768]{1,0:T(1,128)}, f32[1,3072]{1,0:T(1,128)}, /*index=5*/f32[1,768]{1,0:T(1,128)}) custom-call(f32[256,768]{1,0:T(8,128)} %get-tuple-element.54.refs_0_, f32[256,768]{1,0:T(8,128)} %get-tuple-element.55.refs_1_, f32[256,3072]{1,0:T(8,128)} %get-tuple-element.56.refs_2_, ...), custom_call_target="tpu_custom_call" | custom-call | tf_op jit(solution)/shard_map/mlp2/pallas_call | solution.py:274
  185.8 12.1 %att2.1 = (bf16[256,896]{1,0:T(8,128)(2,1)}, bf16[256,3072]{1,0:T(8,128)(2,1)}, f32[1,768]{1,0:T(1,128)}, f32[1,768]{1,0:T(1,128)}, f32[1,2304]{1,0:T(1,128)}, /*index=5*/f32[1,768]{1,0:T(1,128)}) custom-call(f32[256,768]{1,0:T(8,128)} %get-tuple-element.59.refs_0_, f32[256,768]{1,0:T(8,128)} %get-tuple-element.57.refs_1_, ...), custom_call_target="tpu_custom_call" | custom-call | tf_op jit(solution)/shard_map/att2/pallas_call | solution.py:369
  197.9 1.0 slice.117
  198.9 2.0 collective-permute-start.5
  200.8 3.3 collective-permute-done.5
  204.2 1.7 slice_select_fusion
  206.5 3.1 shard_map.319
  210.1 2.0 collective-permute-done.16.theirs_ref
  212.1 2.8 collective-permute-done.17.other_ref
  215.7 3.5 shard_map.320
  219.7 2.7 shard_map.314
  222.9 1.8 collective-permute-done.7.theirs_ref
  224.8 0.8 copy-done.2
  225.6 4.1 %shard_map.315 = bf16[192,3072]{1,0:T(8,128)(2,1)} custom-call(bf16[1152,256]{1,0:T(8,128)(2,1)} %get-tuple-element.76.mine_ref, bf16[1152,256]{1,0:T(8,128)(2,1)} %copy-done.2, bf16[256,3072]{1,0:T(8,128)(2,1)} %get-tuple-element.78.grads_ref, bf16[256,3072]{1,0:T(8,128)(2,1)} %collective-permute-done.8.other_ref), custom_call_target="tpu_custom_call" | custom-call | tf_op jit(solution)/shard_map/pallas_call | solution.py:446
  229.7 1.5 collective-permute-start.9
  232.1 26.0 %collective-permute-done.18.rest_0_ = bf16[768,768]{1,0:T(8,128)(2,1)S(1)} collective-permute-done((bf16[768,768]{1,0:T(8,128)(2,1)}, bf16[768,768]{1,0:T(8,128)(2,1)S(1)}, u32[]{:S(2)}, u32[]{:S(2)}) %collective-permute-start.18) | collective-permute-done | bytes 1179680 | tf_op jit(solution)/shard_map/ppermute | solution.py:650
  258.0 1.0 copy-done.10
  259.1 3.9 shard_map.321
  263.0 1.5 collective-permute-start.19
  267.1 3.5 all-to-all-start
  271.2 11.8 %all-to-all-done = f32[16,1,673]{2,1,0:T(1,128)S(1)} async-done(((f32[16,1,673]{2,1,0:T(1,128)}), f32[16,1,673]{2,1,0:T(1,128)S(1)}, u32[]{:S(2)}, u32[]{:S(2)}) %all-to-all-start) | async-done | bytes 43104 | tf_op jit(solution)/shard_map/all_to_all | solution.py:787
  283.8 2.5 collective-permute-start.2
  286.9 4.2 %shard_map.317 = bf16[192,3072]{1,0:T(8,128)(2,1)} custom-call(bf16[1152,256]{1,0:T(8,128)(2,1)} %get-tuple-element.76.mine_ref, bf16[1152,256]{1,0:T(8,128)(2,1)} %copy-done.2, bf16[256,3072]{1,0:T(8,128)(2,1)} %get-tuple-element.81.grads_ref, bf16[256,3072]{1,0:T(8,128)(2,1)} %collective-permute-done.12.other_ref), custom_call_target="tpu_custom_call" | custom-call | tf_op jit(solution)/shard_map/pallas_call | solution.py:446
  293.0 1.9 collective-permute-start.20
  294.9 4.5 %shard_map.316 = (f32[96,3072]{1,0:T(8,128)}, bf16[96,3072]{1,0:T(8,128)(2,1)}) custom-call(bf16[1152,256]{1,0:T(8,128)(2,1)} %get-tuple-element.76.mine_ref, bf16[1152,256]{1,0:T(8,128)(2,1)} %copy-done.2, bf16[256,3072]{1,0:T(8,128)(2,1)} %get-tuple-element.78.grads_ref, bf16[256,3072]{1,0:T(8,128)(2,1)} %collective-permute-done.8.other_ref, ...), custom_call_target="tpu_custom_call" | custom-call | tf_op jit(solution)/shard_map/pallas_call | solution.py:446
  302.1 6.9 %collective-permute-done.20 = bf16[192,768]{1,0:T(8,128)(2,1)S(1)} collective-permute-done((bf16[192,768]{1,0:T(8,128)(2,1)}, bf16[192,768]{1,0:T(8,128)(2,1)S(1)}, u32[]{:S(2)}, u32[]{:S(2)}) %collective-permute-start.20) | collective-permute-done | bytes 294944 | tf_op jit(solution)/shard_map/ppermute | solution.py:650
  309.0 0.9 add_bitcast_fusion
  309.9 9.1 %collective-permute-done.13.rest_0_ = bf16[192,3072]{1,0:T(8,128)(2,1)S(1)} collective-permute-done((bf16[192,3072]{1,0:T(8,128)(2,1)}, bf16[192,3072]{1,0:T(8,128)(2,1)S(1)}, u32[]{:S(2)}, u32[]{:S(2)}) %collective-permute-start.13) | collective-permute-done | bytes 1179680 | tf_op jit(solution)/shard_map/ppermute | solution.py:650
  319.0 1.0 copy-done.14
  320.0 4.7 %shard_map.318 = (f32[96,3072]{1,0:T(8,128)}, bf16[96,3072]{1,0:T(8,128)(2,1)}) custom-call(bf16[1152,256]{1,0:T(8,128)(2,1)} %get-tuple-element.76.mine_ref, bf16[1152,256]{1,0:T(8,128)(2,1)} %copy-done.2, bf16[256,3072]{1,0:T(8,128)(2,1)} %get-tuple-element.81.grads_ref, bf16[256,3072]{1,0:T(8,128)(2,1)} %collective-permute-done.12.other_ref, ...), custom_call_target="tpu_custom_call" | custom-call | tf_op jit(solution)/shard_map/pallas_call | solution.py:446
  324.7 1.4 collective-permute-start.14
  326.1 1.2 collective-permute-start.11
  327.4 18.0 %collective-permute-done.14 = bf16[96,3072]{1,0:T(8,128)(2,1)S(1)} collective-permute-done((bf16[96,3072]{1,0:T(8,128)(2,1)}, bf16[96,3072]{1,0:T(8,128)(2,1)S(1)}, u32[]{:S(2)}, u32[]{:S(2)}) %collective-permute-start.14) | collective-permute-done | bytes 589856 | tf_op jit(solution)/shard_map/ppermute | solution.py:650
  346.5 12.9 %collective-permute-done.15 = bf16[48,3072]{1,0:T(8,128)(2,1)S(1)} collective-permute-done((bf16[48,3072]{1,0:T(8,128)(2,1)S(1)}, bf16[48,3072]{1,0:T(8,128)(2,1)S(1)}, u32[]{:S(2)}, u32[]{:S(2)}) %collective-permute-start.15) | collective-permute-done | bytes 294944 | tf_op jit(solution)/shard_map/ppermute | solution.py:650
  359.4 0.9 add_bitcast_fusion.1
  360.3 6.8 %thead.1 = f32[256,768]{1,0:T(8,128)} custom-call(s32[1]{0:T(128)} %bitcast.11.refs_0_, bf16[2048,896]{1,0:T(8,128)(2,1)} %all-gather.6.cloned.1.call-done.refs_1_, bf16[256,768]{1,0:T(8,128)(2,1)} %refs_2_.5), custom_call_target="tpu_custom_call" | custom-call | tf_op jit(solution)/shard_map/thead/pallas_call | solution.py:584
  367.7 5.5 %look.1 = (f32[256,768]{1,0:T(8,128)}, f32[64,768]{1,0:T(8,128)}) custom-call(s32[2]{0:T(128)} %pad_add_fusion.base_ref, bf16[2048,896]{1,0:T(8,128)(2,1)} %all-gather.8.cloned.1.call-done.ext_ref), custom_call_target="tpu_custom_call" | custom-call | tf_op jit(solution)/shard_map/look/pallas_call | solution.py:626
  373.2 1.4 fusion
  374.5 1.5 collective-permute-start.6
  376.0 0.8 slice_bitcast_fusion
  376.8 20.5 %collective-permute-done.6 = bf16[320,768]{1,0:T(8,128)(2,1)S(1)} collective-permute-done((bf16[320,768]{1,0:T(8,128)(2,1)S(1)}, bf16[320,768]{1,0:T(8,128)(2,1)S(1)}, u32[]{:S(2)}, u32[]{:S(2)}) %collective-permute-start.6) | collective-permute-done | bytes 491552 | tf_op jit(solution)/shard_map/ppermute | solution.py:802
  398.1 1.0 slice_add_fusion
  (145 shorter events, 17.9 us)
Async XLA Ops:
  7.2 3.2 copy-start
  7.2 67.2 %all-gather.4.cloned.1.call-start = ((), (), s32[]{:S(2)}) async-start(), calls=%async_computation.1 | async-start | bytes 6684672 | tf_op jit(solution)/shard_map/all_gather | solution.py:685
  7.9 352.3 %all-gather.6.cloned.1.call-start = ((), (), s32[]{:S(2)}) async-start(), calls=%async_computation.2 | async-start | bytes 3899392 | tf_op jit(solution)/shard_map/all_gather | solution.py:728
  10.4 1.2 copy-start.18
  10.5 1.3 copy-start.19
  80.5 14.1 %copy-start.31 = (s32[2,128]{1,0:T(2,128)S(1)}, s32[2,128]{1,0:T(2,128)}, u32[]{:S(2)}) copy-start(s32[2,128]{1,0:T(2,128)} %param.20) | copy-start | bytes 3076
  80.5 14.9 %copy-start.29 = (bf16[768]{0:T(1024)(128)(2,1)S(1)}, bf16[768]{0:T(1024)(128)(2,1)}, u32[]{:S(2)}) copy-start(bf16[768]{0:T(1024)(128)(2,1)} %param.24) | copy-start | bytes 4612
  80.5 15.5 %copy-start.30 = (bf16[768]{0:T(1024)(128)(2,1)S(1)}, bf16[768]{0:T(1024)(128)(2,1)}, u32[]{:S(2)}) copy-start(bf16[768]{0:T(1024)(128)(2,1)} %param.25) | copy-start | bytes 4612
  91.0 12.5 %collective-permute-start = (bf16[256,768]{1,0:T(8,128)(2,1)}, bf16[256,768]{1,0:T(8,128)(2,1)S(1)}, u32[]{:S(2)}, u32[]{:S(2)}) collective-permute-start(bf16[256,768]{1,0:T(8,128)(2,1)} %fwd1.1), channel_id=1, source_target_pairs={{0,16},{1,17},{2,18},{3,19},{4,20},{5,21},{6,22},{7,23},{8,24},{9,... | collective-permute-start | bytes 1179656 | tf_op jit(solution)/shard_map/ppermute | solution.py:718
  103.5 0.7 copy-start.16
  130.6 8.8 %collective-permute-start.3 = (bf16[128,896]{1,0:T(8,128)(2,1)S(1)}, bf16[128,896]{1,0:T(8,128)(2,1)S(1)}, u32[]{:S(2)}, u32[]{:S(2)}) collective-permute-start(bf16[128,896]{1,0:T(8,128)(2,1)S(1)} %slice.114), channel_id=1, source_target_pairs={{16,0},{17,1},{18,2},{19,3},{20,4},{21,5},{22,6},{23,7},{24,8},{25... | collective-permute-start | bytes 688136 | tf_op jit(solution)/shard_map/ppermute | solution.py:726
  141.0 226.7 %all-gather.8.cloned.1.call-start = ((), (), s32[]{:S(2)}) async-start(), calls=%async_computation.3 | async-start | bytes 3899392 | tf_op jit(solution)/shard_map/all_gather | solution.py:773
  151.0 23.8 %copy-start.3 = (f32[256,768]{1,0:T(8,128)S(1)}, f32[256,768]{1,0:T(8,128)}, u32[]{:S(2)}) copy-start(f32[256,768]{1,0:T(8,128)} %get-tuple-element.54.refs_0_) | copy-start | bytes 2359300
  163.1 11.7 %collective-permute-start.1 = (bf16[256,768]{1,0:T(8,128)(2,1)}, bf16[256,768]{1,0:T(8,128)(2,1)S(1)}, u32[]{:S(2)}, u32[]{:S(2)}) collective-permute-start(bf16[256,768]{1,0:T(8,128)(2,1)} %att1.1), channel_id=1, source_target_pairs={{16,0},{17,1},{18,2},{19,3},{20,4},{21,5},{22,6},{23,7},{24,8},{25... | collective-permute-start | bytes 1179656 | tf_op jit(solution)/shard_map/ppermute | solution.py:732
  198.9 11.2 %copy-start.5 = (bf16[256,768]{1,0:T(8,128)(2,1)S(1)}, bf16[256,768]{1,0:T(8,128)(2,1)}, u32[]{:S(2)}) copy-start(bf16[256,768]{1,0:T(8,128)(2,1)} %convert_select_fusion.refs_6_.grads_ref) | copy-start | bytes 1179652
  198.9 5.3 %collective-permute-start.5 = (bf16[128,896]{1,0:T(8,128)(2,1)S(1)}, bf16[128,896]{1,0:T(8,128)(2,1)S(1)}, u32[]{:S(2)}, u32[]{:S(2)}) collective-permute-start(bf16[128,896]{1,0:T(8,128)(2,1)S(1)} %slice.117), channel_id=1, source_target_pairs={{0,16},{1,17},{2,18},{3,19},{4,20},{5,21},{6,22},{7,23},{8,24},{9,... | collective-permute-start | bytes 688136 | tf_op jit(solution)/shard_map/ppermute | solution.py:771
  209.6 2.5 collective-permute-start.16
  209.6 15.2 %collective-permute-start.8 = (bf16[256,3072]{1,0:T(8,128)(2,1)}, bf16[256,3072]{1,0:T(8,128)(2,1)}, u32[]{:S(2)}, u32[]{:S(2)}) collective-permute-start(bf16[256,3072]{1,0:T(8,128)(2,1)} %get-tuple-element.78.grads_ref), channel_id=1, source_target_pairs={{0,1},{1,0},{2,3},{3,2},{4,5},{5,4},{6,7},{7,6},{8,9},{9,8},{10,11... | collective-permute-start | bytes 4718600 | tf_op jit(solution)/shard_map/ppermute | solution.py:650
  210.1 4.8 %collective-permute-start.17 = (bf16[256,768]{1,0:T(8,128)(2,1)S(1)}, bf16[256,768]{1,0:T(8,128)(2,1)S(1)}, u32[]{:S(2)}, u32[]{:S(2)}) collective-permute-start(bf16[256,768]{1,0:T(8,128)(2,1)S(1)} %copy-done.5), channel_id=1, source_target_pairs={{0,1},{1,0},{2,3},{3,2},{4,5},{5,4},{6,7},{7,6},{8,9},{9,8},{10,11... | collective-permute-start | bytes 1179656 | tf_op jit(solution)/shard_map/ppermute | solution.py:650
  212.1 2.8 copy-start.6
  214.9 0.8 copy-start.9
  215.7 4.1 copy-start.4
  219.2 38.9 %collective-permute-start.18 = (bf16[768,768]{1,0:T(8,128)(2,1)}, bf16[768,768]{1,0:T(8,128)(2,1)S(1)}, u32[]{:S(2)}, u32[]{:S(2)}) collective-permute-start(bf16[768,768]{1,0:T(8,128)(2,1)} %shard_map.320), channel_id=1, source_target_pairs={{0,2},{1,3},{2,0},{3,1},{4,6},{5,7},{6,4},{7,5},{8,10},{9,11},{10,... | collective-permute-start | bytes 3538952 | tf_op jit(solution)/shard_map/ppermute | solution.py:650
  219.7 67.2 %collective-permute-start.12 = (bf16[256,3072]{1,0:T(8,128)(2,1)S(1)}, bf16[256,3072]{1,0:T(8,128)(2,1)}, u32[]{:S(2)}, u32[]{:S(2)}) collective-permute-start(bf16[256,3072]{1,0:T(8,128)(2,1)S(1)} %copy-done.4), channel_id=1, source_target_pairs={{0,1},{1,0},{2,3},{3,2},{4,5},{5,4},{6,7},{7,6},{8,9},{9,8},{10,11... | collective-permute-start | bytes 4718600 | tf_op jit(solution)/shard_map/ppermute | solution.py:650
  222.4 2.4 collective-permute-start.7
  224.8 0.8 copy-start.2
  225.6 5.5 %copy-start.22 = (f32[1,768]{1,0:T(1,128)S(1)}, f32[1,768]{1,0:T(1,128)}, u32[]{:S(2)}) copy-start(f32[1,768]{1,0:T(1,128)} %get-tuple-element.68) | copy-start | bytes 9220
  225.6 5.6 %copy-start.21 = (f32[1,768]{1,0:T(1,128)S(1)}, f32[1,768]{1,0:T(1,128)}, u32[]{:S(2)}) copy-start(f32[1,768]{1,0:T(1,128)} %get-tuple-element.69) | copy-start | bytes 9220
  229.7 65.2 %collective-permute-start.9 = (bf16[192,3072]{1,0:T(8,128)(2,1)}, bf16[192,3072]{1,0:T(8,128)(2,1)}, u32[]{:S(2)}, u32[]{:S(2)}) collective-permute-start(bf16[192,3072]{1,0:T(8,128)(2,1)} %shard_map.315), channel_id=1, source_target_pairs={{0,2},{1,3},{2,0},{3,1},{4,6},{5,7},{6,4},{7,5},{8,10},{9,11},{10,... | collective-permute-start | bytes 3538952 | tf_op jit(solution)/shard_map/ppermute | solution.py:650
  232.0 32.4 %copy-start.20 = (f32[1,2304]{1,0:T(1,128)S(1)}, f32[1,2304]{1,0:T(1,128)}, u32[]{:S(2)}) copy-start(f32[1,2304]{1,0:T(1,128)} %get-tuple-element.62) | copy-start | bytes 27652
  232.0 32.4 %copy-start.28 = (f32[1,768]{1,0:T(1,128)S(1)}, f32[1,768]{1,0:T(1,128)}, u32[]{:S(2)}) copy-start(f32[1,768]{1,0:T(1,128)} %get-tuple-element.60) | copy-start | bytes 9220
  232.0 32.5 %copy-start.27 = (f32[1,768]{1,0:T(1,128)S(1)}, f32[1,768]{1,0:T(1,128)}, u32[]{:S(2)}) copy-start(f32[1,768]{1,0:T(1,128)} %get-tuple-element.61) | copy-start | bytes 9220
  232.0 32.7 %copy-start.26 = (f32[1,768]{1,0:T(1,128)S(1)}, f32[1,768]{1,0:T(1,128)}, u32[]{:S(2)}) copy-start(f32[1,768]{1,0:T(1,128)} %get-tuple-element.63) | copy-start | bytes 9220
  232.0 32.8 %copy-start.25 = (f32[1,768]{1,0:T(1,128)S(1)}, f32[1,768]{1,0:T(1,128)}, u32[]{:S(2)}) copy-start(f32[1,768]{1,0:T(1,128)} %get-tuple-element.64) | copy-start | bytes 9220
  232.0 32.9 %copy-start.24 = (f32[1,768]{1,0:T(1,128)S(1)}, f32[1,768]{1,0:T(1,128)}, u32[]{:S(2)}) copy-start(f32[1,768]{1,0:T(1,128)} %get-tuple-element.65) | copy-start | bytes 9220
  232.0 33.5 %copy-start.17 = (f32[1,3072]{1,0:T(1,128)S(1)}, f32[1,3072]{1,0:T(1,128)}, u32[]{:S(2)}) copy-start(f32[1,3072]{1,0:T(1,128)} %get-tuple-element.66) | copy-start | bytes 36868
  232.0 34.2 %copy-start.23 = (f32[1,768]{1,0:T(1,128)S(1)}, f32[1,768]{1,0:T(1,128)}, u32[]{:S(2)}) copy-start(f32[1,768]{1,0:T(1,128)} %get-tuple-element.67) | copy-start | bytes 9220
  258.0 1.0 copy-start.10
  263.0 29.2 %collective-permute-start.19 = (bf16[384,768]{1,0:T(8,128)(2,1)}, bf16[384,768]{1,0:T(8,128)(2,1)S(1)}, u32[]{:S(2)}, u32[]{:S(2)}) collective-permute-start(bf16[384,768]{1,0:T(8,128)(2,1)} %get-tuple-element.88), channel_id=1, source_target_pairs={{0,4},{1,5},{2,6},{3,7},{4,0},{5,1},{6,2},{7,3},{8,12},{9,13},{10,... | collective-permute-start | bytes 1769480 | tf_op jit(solution)/shard_map/ppermute | solution.py:650
  267.1 15.9 %all-to-all-start = ((f32[16,1,673]{2,1,0:T(1,128)}), f32[16,1,673]{2,1,0:T(1,128)S(1)}, u32[]{:S(2)}, u32[]{:S(2)}) async-start(f32[16,1,673]{2,1,0:T(1,128)} %all_to_all.6), calls=%async_computation | async-start | bytes 98304 | tf_op jit(solution)/shard_map/all_to_all | solution.py:787
  283.8 16.4 %collective-permute-start.2 = (f32[97]{0:T(128)S(1)}, f32[97]{0:T(128)S(1)}, u32[]{:S(2)}, u32[]{:S(2)}) collective-permute-start(f32[97]{0:T(128)S(1)} %slice.112), channel_id=1, source_target_pairs={{0,16},{16,0},{1,17},{17,1},{2,18},{18,2},{3,19},{19,3},{4,20},{20... | collective-permute-start | bytes 1172 | tf_op jit(solution)/shard_map/ppermute | solution.py:796
  286.9 5.3 %copy-start.11 = (f32[384,768]{1,0:T(8,128)S(1)}, f32[384,768]{1,0:T(8,128)}, u32[]{:S(2)}) copy-start(f32[384,768]{1,0:T(8,128)} %get-tuple-element.87) | copy-start | bytes 3538948
  291.1 27.9 %collective-permute-start.13 = (bf16[192,3072]{1,0:T(8,128)(2,1)}, bf16[192,3072]{1,0:T(8,128)(2,1)S(1)}, u32[]{:S(2)}, u32[]{:S(2)}) collective-permute-start(bf16[192,3072]{1,0:T(8,128)(2,1)} %shard_map.317), channel_id=1, source_target_pairs={{0,2},{1,3},{2,0},{3,1},{4,6},{5,7},{6,4},{7,5},{8,10},{9,11},{10,... | collective-permute-start | bytes 3538952 | tf_op jit(solution)/shard_map/ppermute | solution.py:650
  293.0 16.0 %collective-permute-start.20 = (bf16[192,768]{1,0:T(8,128)(2,1)}, bf16[192,768]{1,0:T(8,128)(2,1)S(1)}, u32[]{:S(2)}, u32[]{:S(2)}) collective-permute-start(bf16[192,768]{1,0:T(8,128)(2,1)} %add_convert_fusion), channel_id=1, source_target_pairs={{0,8},{1,9},{2,10},{3,11},{4,12},{5,13},{6,14},{7,15},{8,0},{9,1},... | collective-permute-start | bytes 884744 | tf_op jit(solution)/shard_map/ppermute | solution.py:650
  299.4 26.6 %collective-permute-start.10 = (bf16[96,3072]{1,0:T(8,128)(2,1)}, bf16[96,3072]{1,0:T(8,128)(2,1)S(1)}, u32[]{:S(2)}, u32[]{:S(2)}) collective-permute-start(bf16[96,3072]{1,0:T(8,128)(2,1)} %get-tuple-element.80), channel_id=1, source_target_pairs={{0,4},{1,5},{2,6},{3,7},{4,0},{5,1},{6,2},{7,3},{8,12},{9,13},{10,... | collective-permute-start | bytes 1769480 | tf_op jit(solution)/shard_map/ppermute | solution.py:650
  309.9 16.2 %copy-start.12 = (f32[96,3072]{1,0:T(8,128)S(1)}, f32[96,3072]{1,0:T(8,128)}, u32[]{:S(2)}) copy-start(f32[96,3072]{1,0:T(8,128)} %get-tuple-element.79) | copy-start | bytes 3538948
  319.0 1.0 copy-start.14
  324.7 20.7 %copy-start.13 = (f32[96,3072]{1,0:T(8,128)S(1)}, f32[96,3072]{1,0:T(8,128)}, u32[]{:S(2)}) copy-start(f32[96,3072]{1,0:T(8,128)} %get-tuple-element.82) | copy-start | bytes 3538948
  324.7 20.7 %collective-permute-start.14 = (bf16[96,3072]{1,0:T(8,128)(2,1)}, bf16[96,3072]{1,0:T(8,128)(2,1)S(1)}, u32[]{:S(2)}, u32[]{:S(2)}) collective-permute-start(bf16[96,3072]{1,0:T(8,128)(2,1)} %get-tuple-element.83), channel_id=1, source_target_pairs={{0,4},{1,5},{2,6},{3,7},{4,0},{5,1},{6,2},{7,3},{8,12},{9,13},{10,... | collective-permute-start | bytes 1769480 | tf_op jit(solution)/shard_map/ppermute | solution.py:650
  326.1 19.6 %collective-permute-start.11 = (bf16[48,3072]{1,0:T(8,128)(2,1)S(1)}, bf16[48,3072]{1,0:T(8,128)(2,1)S(1)}, u32[]{:S(2)}, u32[]{:S(2)}) collective-permute-start(bf16[48,3072]{1,0:T(8,128)(2,1)S(1)} %add_convert_fusion.2), channel_id=1, source_target_pairs={{0,8},{1,9},{2,10},{3,11},{4,12},{5,13},{6,14},{7,15},{8,0},{9,1},... | collective-permute-start | bytes 884744 | tf_op jit(solution)/shard_map/ppermute | solution.py:650
  345.5 13.9 %collective-permute-start.15 = (bf16[48,3072]{1,0:T(8,128)(2,1)S(1)}, bf16[48,3072]{1,0:T(8,128)(2,1)S(1)}, u32[]{:S(2)}, u32[]{:S(2)}) collective-permute-start(bf16[48,3072]{1,0:T(8,128)(2,1)S(1)} %add_convert_fusion.1), channel_id=1, source_target_pairs={{0,8},{1,9},{2,10},{3,11},{4,12},{5,13},{6,14},{7,15},{8,0},{9,1},... | collective-permute-start | bytes 884744 | tf_op jit(solution)/shard_map/ppermute | solution.py:650
  367.1 31.0 %collective-permute-start.4 = (f32[256,768]{1,0:T(8,128)}, f32[256,768]{1,0:T(8,128)S(1)}, u32[]{:S(2)}, u32[]{:S(2)}) collective-permute-start(f32[256,768]{1,0:T(8,128)} %thead.1), channel_id=1, source_target_pairs={{0,16},{16,0},{1,17},{17,1},{2,18},{18,2},{3,19},{19,3},{4,20},{20... | collective-permute-start | bytes 2359304 | tf_op jit(solution)/shard_map/ppermute | solution.py:799
  373.2 24.1 %copy-start.8 = (f32[256,768]{1,0:T(8,128)S(1)}, f32[256,768]{1,0:T(8,128)}, u32[]{:S(2)}) copy-start(f32[256,768]{1,0:T(8,128)} %get-tuple-element.73) | copy-start | bytes 2359300
  373.2 24.1 %copy-start.15 = (f32[64,768]{1,0:T(8,128)S(1)}, f32[64,768]{1,0:T(8,128)}, u32[]{:S(2)}) copy-start(f32[64,768]{1,0:T(8,128)} %get-tuple-element.74) | copy-start | bytes 589828
  374.5 22.8 %collective-permute-start.6 = (bf16[320,768]{1,0:T(8,128)(2,1)S(1)}, bf16[320,768]{1,0:T(8,128)(2,1)S(1)}, u32[]{:S(2)}, u32[]{:S(2)}) collective-permute-start(bf16[320,768]{1,0:T(8,128)(2,1)S(1)} %fusion), channel_id=1, source_target_pairs={{0,16},{16,0},{1,17},{17,1},{2,18},{18,2},{3,19},{19,3},{4,20},{20... | collective-permute-start | bytes 1474568 | tf_op jit(solution)/shard_map/ppermute | solution.py:802
  376.8 21.3 %copy-start.7 = (f32[256,768]{1,0:T(8,128)S(1)}, f32[256,768]{1,0:T(8,128)}, u32[]{:S(2)}) copy-start(f32[256,768]{1,0:T(8,128)} %thead.1) | copy-start | bytes 2359300
  397.4 1.7 copy-start.1
Sparse Core Ops, SparseCore 0:
  10.3 64.1 all-gather.3
  141.1 45.4 all-gather.5
  206.0 57.7 all-gather.7
